TPU v7x, 32 devices: a whole 2x2x4 slice. The times are simulated.
32 devices in a mesh: dp: 8 (over z, x), tensor: 4 (over y, core).
Axes of the slice: x: 2, y: 2, z: 4, core: 2. Of those that a mesh axis runs over, the one named last changes fastest.
Arguments:
- block_input: float32 [8192, 768], P(('dp', 'tensor')), may hold values from -40 to 40
- norm_gain: float32 [768], replicated, may hold values from 0.5 to 1.5
- zx_weight: bfloat16 [2, 768, 1536], P(None, 'dp', 'tensor'), may hold values from -0.21875 to 0.21875
- bc_weight: bfloat16 [768, 256], P('dp'), may hold values from -0.21875 to 0.21875
- dt_weight: bfloat16 [768, 24], P('dp', 'tensor'), may hold values from -0.21875 to 0.21875
- conv_x_weight: float32 [4, 1536], replicated, may hold values from -3 to 3
- conv_x_bias: float32 [1536], replicated, may hold values from -0.5 to 0.5
- conv_bc_weight: float32 [4, 256], replicated, may hold values from -3 to 3
- conv_bc_bias: float32 [256], replicated, may hold values from -0.5 to 0.5
- dt_bias: float32 [24], replicated, may hold values from -7 to -2
- decay_log: float32 [24], replicated, may hold values from 0 to 1.5
- skip_gain: float32 [24], replicated, may hold values from 0.2 to 1
- gate_gain: float32 [1536], replicated, may hold values from 0.5 to 1.5
- out_weight: bfloat16 [1536, 768], P('tensor', 'dp'), may hold values from -0.15625 to 0.15625
- segments: int32 [8192], P('dp'), may hold values from 0 to 3, never falling along the last dimension, each value on 1 to 4096 neighbouring positions
- cotangent: float32 [8192, 768], P(('dp', 'tensor')), may hold values from -6 to 6
Outputs:
- output: float32 [8192, 768], P(('dp', 'tensor'))
- grad_input: float32 [8192, 768], P(('dp', 'tensor'))
- grad_norm_gain: float32 [768], replicated
- grad_zx_weight: float32 [2, 768, 1536], P(None, 'dp', 'tensor')
- grad_bc_weight: float32 [768, 256], P('dp')
- grad_dt_weight: float32 [768, 24], P('dp', 'tensor')
- grad_conv_x_weight: float32 [4, 1536], replicated
- grad_conv_x_bias: float32 [1536], replicated
- grad_conv_bc_weight: float32 [4, 256], replicated
- grad_conv_bc_bias: float32 [256], replicated
- grad_dt_bias: float32 [24], replicated
- grad_decay_log: float32 [24], replicated
- grad_skip_gain: float32 [24], replicated
- grad_gate_gain: float32 [1536], replicated
- grad_out_weight: float32 [1536, 768], P('tensor', 'dp')
Inputs may be any that keep to these rules, and one draw needn't show every extreme that they name: `segments`: segment numbers never fall along the tokens and every number from 0 up occurs; a number covers at most 4096 consecutive tokens, and one covers exactly that many.
All inputs are finite; a program needn't handle non-finite values.
Results may differ from a plain program's by a relative error of at most 0.012.
The roundings to bfloat16 on the way count: a program that leaves them out, or rounds other values in their place, can miss the bound.
Values may be sent and summed in bfloat16 or wider, within the bound.
A program may use at most 256 MiB of HBM per device.

v0:
```python
import jax
import jax.numpy as jnp
from jax import lax
from jax.sharding import PartitionSpec as P

GROUP = 256
LENGTH = 4096


EPSILON = 1e-05
exact_prec = lax.Precision.HIGHEST


def from_behind(block, axis, distance):
    devices = range(lax.axis_size(axis))
    route = [(i - distance, i) for i in devices if i - distance in devices]
    return lax.ppermute(block, axis, route)


def prefix(value, axis, join, neutral, backward):
    count, mine = (lax.axis_size(axis), lax.axis_index(axis))
    pieces = jax.tree.map(lambda part: lax.all_gather(part, axis), value)
    if backward:
        pieces = jax.tree.map(lambda part: part[::-1], pieces)
        mine = count - 1 - mine
    running = jax.tree.map(
        lambda part, zero: jnp.full_like(part, 0) + jnp.asarray(zero, part.dtype), value, neutral
    )

    def turn(position, running):
        longer = join(running, jax.tree.map(lambda part: part[position], pieces))
        return jax.tree.map(lambda new, old: jnp.where(position < mine, new, old), longer, running)

    return lax.fori_loop(0, count - 1, turn, running)


def dot_wide(left, right):
    return jnp.dot(left, right, preferred_element_type=jnp.float32)


def ssd_groups(inner_x, state_b, state_c, step_dt, decay_log, resets, start_state):
    tokens_here = inner_x.shape[0]
    blocks = tokens_here // GROUP

    def to_blocks(array):
        return array.reshape((blocks, GROUP) + array.shape[1:])

    rate = -jnp.exp(decay_log)
    index = jnp.arange(GROUP, dtype=jnp.int32)
    lower = index[:, None] >= index[None, :]

    def advance(state, pieces):
        block_x, block_b, block_c, block_dt, block_reset = pieces
        log_decay = block_dt * rate[None, :]
        cumul = jnp.cumsum(log_decay, axis=0)
        run_id = jnp.cumsum(block_reset)
        same_run = (run_id[:, None] == run_id[None, :]) & lower
        spread = cumul[:, None, :] - cumul[None, :, :]
        mask_three = same_run[:, :, None]
        decay = jnp.where(mask_three, jnp.exp(jnp.where(mask_three, spread, 0.0)), 0.0)
        scores = jnp.dot(block_c, block_b.T, precision=exact_prec)
        weighted_x = block_x * block_dt[:, :, None]
        mixing = decay * scores[:, :, None]
        within = jnp.einsum("tsh,shp->thp", mixing, weighted_x, precision=exact_prec)
        keep_first = (run_id == 0).astype(jnp.float32)
        inflow_w = jnp.exp(cumul) * keep_first[:, None]
        carried = (
            jnp.einsum("tn,hpn->thp", block_c, state, precision=exact_prec) * inflow_w[:, :, None]
        )
        tail_w = decay[GROUP - 1]
        new_state = state * inflow_w[GROUP - 1][:, None, None] + jnp.einsum(
            "sh,shp,sn->hpn", tail_w, weighted_x, block_b, precision=exact_prec
        )
        return (new_state, within + carried)

    final, outputs = lax.scan(
        advance,
        start_state,
        (
            to_blocks(inner_x),
            to_blocks(state_b),
            to_blocks(state_c),
            to_blocks(step_dt),
            to_blocks(resets),
        ),
    )
    return (outputs.reshape(inner_x.shape), final)


def conv_apply(pre_ext, kernel, offsets, validity):
    length = validity.shape[0]
    total = jnp.broadcast_to(offsets[None, :], (length, offsets.shape[0]))
    for offset in range(kernel.shape[0]):
        total = (
            total
            + kernel[offset][None, :]
            * pre_ext[offset : offset + length]
            * validity[:, offset : offset + 1]
        )
    return jax.nn.silu(total)


def valid_and_resets(seg_ext, pos_ext, width_back):
    length = seg_ext.shape[0] - width_back
    own_seg = seg_ext[width_back:]
    own_pos = pos_ext[width_back:]
    columns = []
    for offset in range(width_back + 1):
        same = (seg_ext[offset : offset + length] == own_seg) & (
            pos_ext[offset : offset + length] // LENGTH == own_pos // LENGTH
        )
        columns.append(same.astype(jnp.float32))
    validity = jnp.stack(columns, axis=1)
    resets = (
        (seg_ext[width_back - 1 : width_back - 1 + length] != own_seg) | (own_pos % LENGTH == 0)
    ).astype(jnp.float32)
    return (validity, resets)


def entry_weights(step_dt, decay_log, resets):
    cumul = jnp.cumsum(step_dt * (-jnp.exp(decay_log))[None, :], axis=0)
    keep_first = (jnp.cumsum(resets) == 0).astype(jnp.float32)
    weights_in = jnp.exp(cumul) * keep_first[:, None]
    return (weights_in, weights_in[-1])


def join_states(earlier, later):
    return (earlier[0] * later[0], later[0][:, None, None] * earlier[1] + later[1])


def place_slice(piece, total_len, start, axis):
    full_shape = list(piece.shape)
    full_shape[axis] = total_len
    return lax.dynamic_update_slice_in_dim(
        jnp.zeros(tuple(full_shape), jnp.float32), piece, start, axis
    )


def fetch_weights(zx_part, bc_part, dt_part, out_part):
    return (
        lax.all_gather(zx_part, "dp", axis=1, tiled=True),
        lax.all_gather(bc_part, "dp", axis=0, tiled=True),
        lax.all_gather(dt_part, "dp", axis=0, tiled=True),
        lax.all_gather(out_part, "dp", axis=1, tiled=True),
    )


def per_device(
    block_input,
    norm_gain,
    zx_weight,
    bc_weight,
    dt_weight,
    conv_x_weight,
    conv_x_bias,
    conv_bc_weight,
    conv_bc_bias,
    dt_bias,
    decay_log,
    skip_gain,
    gate_gain,
    out_weight,
    segments,
    cotangent,
):
    tensor_count = lax.axis_size("tensor")
    tensor_index = lax.axis_index("tensor")
    data_index = lax.axis_index("dp")
    token_count = segments.shape[0]
    row_count = block_input.shape[0]
    heads_here = dt_weight.shape[1]
    inner_here = out_weight.shape[0]
    head_size = inner_here // heads_here
    inner_total = inner_here * tensor_count
    heads_total = heads_here * tensor_count
    width_back = conv_x_weight.shape[0] - 1
    head_start = tensor_index * heads_here
    inner_start = tensor_index * inner_here
    local_bias = lax.dynamic_slice_in_dim(dt_bias, head_start, heads_here)
    local_log = lax.dynamic_slice_in_dim(decay_log, head_start, heads_here)
    local_skip = lax.dynamic_slice_in_dim(skip_gain, head_start, heads_here)
    local_gate_gain = lax.dynamic_slice_in_dim(gate_gain, inner_start, inner_here)
    conv_weight = jnp.concatenate(
        [lax.dynamic_slice_in_dim(conv_x_weight, inner_start, inner_here, 1), conv_bc_weight],
        axis=1,
    )
    conv_bias = jnp.concatenate(
        [lax.dynamic_slice_in_dim(conv_x_bias, inner_start, inner_here), conv_bc_bias]
    )
    full_zx, full_bc, full_dt, full_out = fetch_weights(zx_weight, bc_weight, dt_weight, out_weight)
    rstd = lax.rsqrt(jnp.mean(block_input * block_input, axis=-1, keepdims=True) + EPSILON)
    normed_rows = (block_input * rstd * norm_gain).astype(jnp.bfloat16)
    normed = lax.all_gather(normed_rows, "tensor", axis=0, tiled=True)
    gate_in = dot_wide(normed, full_zx[0])
    pre = jnp.concatenate([dot_wide(normed, full_zx[1]), dot_wide(normed, full_bc)], axis=1).astype(
        jnp.bfloat16
    )
    raw_dt = dot_wide(normed, full_dt) + local_bias
    step_dt = jax.nn.softplus(raw_dt)
    tail_start = token_count - width_back
    tail_vals, tail_ids = from_behind(
        (pre[tail_start:], segments[tail_start:].astype(jnp.bfloat16)), "dp", 1
    )
    seg_ext = jnp.concatenate([tail_ids.astype(jnp.float32), segments.astype(jnp.float32)])
    pos_ext = (
        data_index * token_count
        - width_back
        + jnp.arange(token_count + width_back, dtype=jnp.int32)
    )
    validity, resets = valid_and_resets(seg_ext, pos_ext, width_back)
    pre_ext = jnp.concatenate([tail_vals, pre], axis=0).astype(jnp.float32)
    activ = conv_apply(pre_ext, conv_weight, conv_bias, validity).astype(jnp.bfloat16)
    inner_x = activ[:, :inner_here].astype(jnp.float32).reshape(token_count, heads_here, head_size)
    state_size = (activ.shape[1] - inner_here) // 2
    state_b = activ[:, inner_here : inner_here + state_size].astype(jnp.float32)
    state_c = activ[:, inner_here + state_size :].astype(jnp.float32)
    zero_state = jnp.zeros((heads_here, head_size, state_size), jnp.float32)

    def mixer(arg_x, arg_b, arg_c, arg_dt, arg_log):
        return ssd_groups(arg_x, arg_b, arg_c, arg_dt, arg_log, resets, zero_state)

    local_y, local_end = mixer(inner_x, state_b, state_c, step_dt, local_log)
    inflow_w, device_decay = entry_weights(step_dt, local_log, resets)
    carried = prefix(
        (device_decay, local_end),
        "dp",
        join_states,
        (jnp.ones_like(device_decay), jnp.zeros_like(local_end)),
        False,
    )
    entry_state = carried[1]

    def inflow(arg_c, arg_dt, arg_log):
        weights_in, decay_in = entry_weights(arg_dt, arg_log, resets)
        arrived_y = (
            jnp.einsum("tn,hpn->thp", arg_c, entry_state, precision=exact_prec)
            * weights_in[:, :, None]
        )
        return (arrived_y, decay_in[:, None, None] * entry_state)

    arrived, passed_on = inflow(state_c, step_dt, local_log)
    mixed_three = local_y + arrived + local_skip[None, :, None] * inner_x
    mixed = mixed_three.reshape(token_count, inner_here)
    gate_act = jax.nn.silu(gate_in)
    gated = mixed * gate_act
    total_sq = lax.psum(jnp.sum(gated * gated, axis=1), "tensor")
    rstd_gate = lax.rsqrt(total_sq / inner_total + EPSILON)[:, None]
    normed_out = (gated * rstd_gate * local_gate_gain).astype(jnp.bfloat16)
    branch = lax.psum_scatter(
        dot_wide(normed_out, full_out), "tensor", scatter_dimension=0, tiled=True
    )
    result = block_input + branch
    cot_rows = cotangent.astype(jnp.bfloat16)
    cot_full = lax.all_gather(cot_rows, "tensor", axis=0, tiled=True)
    d_normed_out = dot_wide(cot_full, full_out.T)
    g_out = dot_wide(normed_out.T, cot_full)
    g_gate_local = jnp.sum(d_normed_out * gated * rstd_gate, axis=0)
    scaled = local_gate_gain * d_normed_out
    gate_dots = lax.psum(jnp.sum(scaled * gated, axis=1), "tensor")
    d_gated = rstd_gate * scaled - gated * rstd_gate**3 * (gate_dots / inner_total)[:, None]
    sigm = jax.nn.sigmoid(gate_in)
    d_mixed = d_gated * gate_act
    d_gate_in = (d_gated * mixed * sigm * (1.0 + gate_in * (1.0 - sigm))).astype(jnp.bfloat16)
    d_mixed_three = d_mixed.reshape(token_count, heads_here, head_size)
    g_skip_local = jnp.sum(d_mixed_three * inner_x, axis=(0, 2))
    state_cot = jnp.einsum("th,thp,tn->hpn", inflow_w, d_mixed_three, state_c, precision=exact_prec)
    backward_chain = prefix(
        (device_decay, state_cot),
        "dp",
        join_states,
        (jnp.ones_like(device_decay), jnp.zeros_like(state_cot)),
        True,
    )
    exit_cot = backward_chain[1]
    replay_out, mixer_back = jax.vjp(mixer, inner_x, state_b, state_c, step_dt, local_log)
    replay_in, inflow_back = jax.vjp(inflow, state_c, step_dt, local_log)
    d_x, d_b, d_c, d_step, d_log = mixer_back((d_mixed_three, exit_cot))
    d_c_in, d_step_in, d_log_in = inflow_back((d_mixed_three, exit_cot))
    d_x = d_x + local_skip[None, :, None] * d_mixed_three
    d_c = d_c + d_c_in
    d_step = d_step + d_step_in
    d_log = d_log + d_log_in
    d_b, d_c = lax.psum((d_b, d_c), "tensor")
    d_activ = jnp.concatenate([d_x.reshape(token_count, inner_here), d_b, d_c], axis=1)

    def conv_part(values, kernel, offsets):
        return conv_apply(values, kernel, offsets, validity)

    conv_out, conv_back = jax.vjp(conv_part, pre_ext, conv_weight, conv_bias)
    d_pre_ext, g_conv_w, g_conv_b = conv_back(d_activ)
    from_next = from_behind(d_pre_ext[:width_back], "dp", -1)
    d_pre_own = d_pre_ext[width_back:]
    d_pre = jnp.concatenate(
        [d_pre_own[:tail_start], d_pre_own[tail_start:] + from_next], axis=0
    ).astype(jnp.bfloat16)
    d_raw = d_step * jax.nn.sigmoid(raw_dt)
    g_dt_bias_local = jnp.sum(d_raw, axis=0)
    d_raw_b = d_raw.astype(jnp.bfloat16)
    partial_rows = (
        dot_wide(d_gate_in, full_zx[0].T)
        + dot_wide(d_pre[:, :inner_here], full_zx[1].T)
        + dot_wide(d_raw_b, full_dt.T)
    )
    own_bc = lax.dynamic_slice_in_dim(d_pre[:, inner_here:], tensor_index * row_count, row_count, 0)
    d_normed_rows = lax.psum_scatter(
        partial_rows, "tensor", scatter_dimension=0, tiled=True
    ) + dot_wide(own_bc, full_bc.T)
    g_zx = jnp.stack([dot_wide(normed.T, d_gate_in), dot_wide(normed.T, d_pre[:, :inner_here])])
    g_bc = dot_wide(normed.T, d_pre[:, inner_here:])
    g_dt = dot_wide(normed.T, d_raw_b)
    grad_zx, grad_bc, grad_dt, grad_out = (
        lax.psum_scatter(g_zx, "dp", scatter_dimension=1, tiled=True),
        lax.psum_scatter(g_bc, "dp", scatter_dimension=0, tiled=True),
        lax.psum_scatter(g_dt, "dp", scatter_dimension=0, tiled=True),
        lax.psum_scatter(g_out, "dp", scatter_dimension=1, tiled=True),
    )
    scaled_in = norm_gain * d_normed_rows
    g_norm_local = jnp.sum(d_normed_rows * block_input * rstd, axis=0)
    grad_input = (
        cotangent
        + rstd * scaled_in
        - block_input * rstd**3 * jnp.mean(scaled_in * block_input, axis=-1, keepdims=True)
    )
    small_sums = lax.psum(
        (
            g_norm_local,
            place_slice(g_conv_w[:, :inner_here], inner_total, inner_start, 1),
            place_slice(g_conv_b[:inner_here], inner_total, inner_start, 0),
            g_conv_w[:, inner_here:] / tensor_count,
            g_conv_b[inner_here:] / tensor_count,
            place_slice(g_dt_bias_local, heads_total, head_start, 0),
            place_slice(d_log, heads_total, head_start, 0),
            place_slice(g_skip_local, heads_total, head_start, 0),
            place_slice(g_gate_local, inner_total, inner_start, 0),
        ),
        ("dp", "tensor"),
    )
    grad_norm, grad_cxw, grad_cxb, grad_cbw, grad_cbb, grad_dtb, grad_log, grad_skip, grad_gate = (
        small_sums
    )
    return (
        result,
        grad_input,
        grad_norm,
        grad_zx,
        grad_bc,
        grad_dt,
        grad_cxw,
        grad_cxb,
        grad_cbw,
        grad_cbb,
        grad_dtb,
        grad_log,
        grad_skip,
        grad_gate,
        grad_out,
    )


def solution(mesh):
    in_specs = (
        P(("dp", "tensor"), None),
        P(),
        P(None, "dp", "tensor"),
        P("dp", None),
        P("dp", "tensor"),
        P(),
        P(),
        P(),
        P(),
        P(),
        P(),
        P(),
        P(),
        P("tensor", "dp"),
        P("dp"),
        P(("dp", "tensor"), None),
    )
    out_specs = (
        P(("dp", "tensor"), None),
        P(("dp", "tensor"), None),
        P(),
        P(None, "dp", "tensor"),
        P("dp", None),
        P("dp", "tensor"),
        P(),
        P(),
        P(),
        P(),
        P(),
        P(),
        P(),
        P(),
        P("tensor", "dp"),
    )
    return jax.shard_map(
        per_device, mesh=mesh, in_specs=in_specs, out_specs=out_specs, check_vma=False
    )
```

profile of v0, /device:TPU:0, one launch (start us, length us, event | category | flops | bytes accessed | tf_op | source)
XLA Modules:
  0.0 1100.1 jit_solution(5276489474987137423)
XLA Ops:
  17.0 26.6 %all-gather.2 = bf16[8,96,6]{1,2,0:T(8,128)(2,1)S(1)} all-gather(bf16[1,96,6]{1,2,0:T(8,128)(2,1)S(1)} %bitcast.690), channel_id=1, replica_groups=mesh['dp'=8,'tensor'=4] {'dp'}, dimensions={0}, use_global_device_ids=true | all-gather | bytes 10368 | tf_op jit(solution)/shard_map/all_gather | solution.py:143
  45.3 31.3 %all_gather.37 = bf16[768,256]{1,0:T(8,128)(2,1)S(1)} all-gather(bf16[96,256]{1,0:T(8,128)(2,1)S(1)} %copy-done.61), channel_id=1, replica_groups=mesh['dp'=8,'tensor'=4] {'dp'}, dimensions={0}, use_global_device_ids=true | all-gather | bytes 442368 | tf_op jit(solution)/shard_map/all_gather | solution.py:142
  103.9 101.7 %while.114 = (s32[]{:T(128)}, f32[6,64,128]{2,1,0:T(8,128)}, f32[4,256,6,64]{1,0,3,2:T(4,128)}, f32[4,256,6]{1,2,0:T(8,128)}, f32[6]{0:T(128)}, /*index=5*/f32[4...) while((s32[]{:T(128)}, f32[6,64,128]{2,1,0:T(8,128)}, ...), condition=%wide.region_6.7_spmd.clone, body=%wide.region_1.6_spmd.clone.sunk | while | flops 708513280 | bytes 11361720 | solution.py:76
  116.4 9.5 dynamic_update_slice.252
  141.8 9.5 dynamic_update_slice.252
  167.3 9.5 dynamic_update_slice.252
  192.8 9.5 dynamic_update_slice.252
  209.4 37.2 %all_gather.41 = bf16[384,768]{0,1:T(8,128)(2,1)} all-gather(bf16[384,96]{0,1:T(8,128)(2,1)} %param.39), channel_id=1, replica_groups=mesh['dp'=8,'tensor'=4] {'dp'}, dimensions={1}, use_global_device_ids=true | all-gather | bytes 663552 | tf_op jit(solution)/shard_map/all_gather | solution.py:144
  257.4 19.9 %all-gather.3 = f32[8,1,6]{2,1,0:T(1,128)S(1)} all-gather(f32[1,1,6]{2,1,0:T(1,128)S(1)} %bitcast.691), channel_id=1, replica_groups=mesh['dp'=8,'tensor'=4] {'dp'}, dimensions={0}, use_global_device_ids=true | all-gather | bytes 216 | tf_op jit(solution)/shard_map/all_gather | solution.py:22
  280.9 7.4 while.115
  295.6 5.7 psum.91
  306.1 5.7 psum.92
  322.4 107.0 %while.117 = (s32[]{:T(128)}, f32[6,64,128]{2,1,0:T(8,128)S(1)}, pred[4,256,256,6]{2,1,3,0:T(32,128)(4,1)}, f32[4,256,256,6]{2,1,3,0:T(8,128)}, f32[4,128,256]{1...) while((s32[]{:T(128)}, f32[6,64,128]{2,1,0:T(8,128)S(1)}, ...), condition=%wide.region_25.26_spmd.clone, body=%wide.region_20.25_spmd.clone.sunk | while | flops 405398272 | bytes 10158093 | solution.py:76
  440.7 12.1 %while.116 = (s32[]{:T(128)}, f32[6,64,128]{2,1,0:T(8,128)S(1)}, s32[]{:T(128)}, f32[8,6]{1,0:T(8,128)}, f32[8,6,64,128]{3,2,1,0:T(8,128)}, /*index=5*/s32[]{:T(128)}, s32[]{:T(128)}) while((s32[]{:T(128)}, f32[6,64,128]{2,1,0:T(8,128)S(1)}, s32[]{:T(128)}, f32[8,6]{1,0:T(8,128)}, f32[8,6,64,128]{3,2,1,0:T(8,128)}, ...), condition=%wide.region_19.20_spmd.clone, body=%wide.region_18.19_spmd.clone.sunk | while | flops 196612 | bytes 590001 | solution.py:34
  457.2 229.4 %while.118 = (s32[]{:T(128)}, f32[6]{0:T(128)}, f32[6,64,128]{2,1,0:T(8,128)S(1)}, f32[4,256,6,64]{1,0,3,2:T(4,128)}, f32[4,256,128]{2,1,0:T(8,128)}, /*index=5*...) while((s32[]{:T(128)}, f32[6]{0:T(128)}, ...), condition=%wide.region_36.37_spmd.clone, body=%wide.region_26.36_spmd.clone.sunk | while | flops 1414307328 | bytes 18141048 | solution.py:76
  466.6 9.5 dynamic_update_slice.267
  488.4 8.2 reduce-window.143
  523.9 9.5 dynamic_update_slice.267
  545.7 8.2 reduce-window.143
  581.3 9.5 dynamic_update_slice.267
  603.1 8.2 reduce-window.143
  638.6 9.5 dynamic_update_slice.267
  660.4 8.2 reduce-window.143
  697.5 7.7 reduce-window.113
  712.6 26.5 %all-reduce.15.cloned.1.call-done = (f32[1024,128]{0,1:T(8,128)}, f32[1024,128]{0,1:T(8,128)}) async-done(((f32[1024,128]{0,1:T(8,128)}, f32[1024,128]{0,1:T(8,128)}), (f32[1024,128]{0,1:T(8,128)}, f32[1024,128]{0,1:T(8,128)})) %all-reduce.15.cloned.1.call-update) | async-done | bytes 1048592 | tf_op jit(solution)/shard_map/psum | solution.py:283
  750.0 7.3 collective-permute-done.2
  779.1 26.0 %reduce-scatter.19.cloned.1.call-done = f32[96,6]{1,0:T(8,128)} async-done(((f32[768,6]{1,0:T(8,128)}), f32[96,6]{1,0:T(8,128)}) %reduce-scatter.19.cloned.1.call-update) | async-done | bytes 2320
  807.0 37.5 %reduce-scatter.11.cloned.1.call-done = f32[256,768]{1,0:T(8,128)} async-done(((f32[1024,768]{1,0:T(8,128)}), f32[256,768]{1,0:T(8,128)}) %reduce-scatter.11.cloned.1.call-update) | async-done | bytes 786448 | tf_op jit(solution)/shard_map/reduce_scatter | solution.py:305
  847.1 41.0 %all-reduce.11 = (f32[768]{0:T(1024)}, f32[4,1536]{1,0:T(4,128)}, f32[1536]{0:T(1024)}, f32[4,256]{1,0:T(4,128)}, f32[256]{0:T(256)}, /*index=5*/f32[24]{0:T(128)}, f32[24]{0:T(128)}, f32[24]{0:T(128)}, f32[1536]{0:T(1024)}) all-reduce(f32[768]{0:T(1024)S(1)} %get-tuple-element.1935, ...), channel_id=1, replica_groups=mesh['dp'=8,'tensor'=4] {'dp','tensor'}, use_global_device_ids=true, to_apply=%region_46.47 | all-reduce | flops 11336 | bytes 90688 | tf_op jit(solution)/shard_map/psum | solution.py:324
  891.2 62.8 %reduce-scatter.17.cloned.1.call-done = f32[384,96]{0,1:T(8,128)} async-done(((f32[384,768]{0,1:T(8,128)}), f32[384,96]{0,1:T(8,128)}) %reduce-scatter.17.cloned.1.call-update) | async-done | bytes 147472 | tf_op jit(solution)/shard_map/reduce_scatter | solution.py:315
  954.0 66.2 %reduce-scatter.15.cloned.1.call-done = f32[96,256]{1,0:T(8,128)} async-done(((f32[768,256]{1,0:T(8,128)}), f32[96,256]{1,0:T(8,128)}) %reduce-scatter.15.cloned.1.call-update) | async-done | bytes 98320 | tf_op jit(solution)/shard_map/reduce_scatter | solution.py:313
  1020.2 72.5 %reduce-scatter.13.cloned.1.call-done = f32[2,96,384]{2,1,0:T(8,128)} async-done(((f32[2,768,384]{2,1,0:T(8,128)}), f32[2,96,384]{2,1,0:T(8,128)}) %reduce-scatter.13.cloned.1.call-update) | async-done | bytes 294928 | tf_op jit(solution)/shard_map/reduce_scatter | solution.py:312
  (857 shorter events, 499.6 us)
Async XLA Ops:
  7.2 37.4 %copy-start = (f32[4,1536]{1,0:T(4,128)S(1)}, f32[4,1536]{1,0:T(4,128)}, u32[]{:S(2)}) copy-start(f32[4,1536]{1,0:T(4,128)} %param.31) | copy-start | bytes 73732
  7.3 38.0 %copy-start.90 = (f32[256]{0:T(256)S(1)}, f32[256]{0:T(256)}, u32[]{:S(2)}) copy-start(f32[256]{0:T(256)} %param.34) | copy-start | bytes 3076
  7.3 38.0 %copy-start.61 = (bf16[96,256]{1,0:T(8,128)(2,1)S(1)}, bf16[96,256]{1,0:T(8,128)(2,1)}, u32[]{:S(2)}) copy-start(bf16[96,256]{1,0:T(8,128)(2,1)} %param.29) | copy-start | bytes 147460
  7.3 70.1 %all-gather.12.cloned.1.call-start = ((), (), s32[]{:S(2)}) async-start(), calls=%async_computation.7 | async-start | bytes 1327104 | tf_op jit(solution)/shard_map/all_gather | solution.py:141
  8.0 69.4 %all-gather.10.cloned.1.call-start = ((), (), s32[]{:S(2)}) async-start(), calls=%async_computation.6 | async-start | bytes 1966080 | tf_op jit(solution)/shard_map/all_gather | solution.py:193
  11.9 268.9 %all-gather.16.cloned.1.call-start = ((), (), s32[]{:S(2)}) async-start(), calls=%async_computation.14 | async-start | bytes 1769472 | tf_op jit(solution)/shard_map/all_gather | solution.py:22
  12.1 64.5 %collective-permute-start = (bf16[3]{0:T(256)(128)(2,1)S(1)}, bf16[3]{0:T(256)(128)(2,1)S(1)}, u32[]{:S(2)}, u32[]{:S(2)}) collective-permute-start(bf16[3]{0:T(256)(128)(2,1)S(1)} %slice.216), channel_id=1, source_target_pairs={{0,4},{4,8},{8,12},{12,16},{16,20},{20,24},{24,28},{1,5},{5,9},{9,... | collective-permute-start | bytes 26 | tf_op jit(solution)/shard_map/ppermute | solution.py:17
  43.7 38.5 %copy-start.45 = (bf16[768,6]{0,1:T(8,128)(2,1)}, bf16[768,6]{0,1:T(8,128)(2,1)S(1)}, u32[]{:S(2)}) copy-start(bf16[768,6]{0,1:T(8,128)(2,1)S(1)} %reshape.601) | copy-start | bytes 27652
  44.6 42.1 %copy-start.67 = (f32[640]{0:T(1024)}, f32[640]{0:T(1024)S(1)}, u32[]{:S(2)}) copy-start(f32[640]{0:T(1024)S(1)} %get-tuple-element.1937) | copy-start | bytes 7684
  44.6 42.1 %copy-start.69 = (f32[640]{0:T(1024)}, f32[640]{0:T(1024)S(1)}, u32[]{:S(2)}) copy-start(f32[640]{0:T(1024)S(1)} %get-tuple-element.1938) | copy-start | bytes 7684
  44.6 42.1 %copy-start.71 = (f32[640]{0:T(1024)}, f32[640]{0:T(1024)S(1)}, u32[]{:S(2)}) copy-start(f32[640]{0:T(1024)S(1)} %get-tuple-element.1939) | copy-start | bytes 7684
  44.6 42.1 %copy-start.73 = (f32[640]{0:T(1024)}, f32[640]{0:T(1024)S(1)}, u32[]{:S(2)}) copy-start(f32[640]{0:T(1024)S(1)} %get-tuple-element.1940) | copy-start | bytes 7684
  80.7 5.3 collective-permute-start.1
  205.6 41.7 %copy-start.63 = (f32[1024]{0:T(1024)S(1)}, f32[1024]{0:T(1024)}, u32[]{:S(2)}) copy-start(f32[1024]{0:T(1024)} %copy-done.62) | copy-start | bytes 12292
  205.6 95.8 %all-gather.14.cloned.1.call-start = ((), (), s32[]{:S(2)}) async-start(), calls=%async_computation.9 | async-start | bytes 1966080 | tf_op jit(solution)/shard_map/all_gather | solution.py:254
  207.8 230.2 %all-gather.18.cloned.1.call-start = ((), (), s32[]{:S(2)}) async-start(), calls=%async_computation.15 | async-start | bytes 1769472 | tf_op jit(solution)/shard_map/all_gather | solution.py:22
  208.6 39.0 %copy-start.87 = (f32[6]{0:T(128)}, f32[6]{0:T(128)S(1)}, u32[]{:S(2)}) copy-start(f32[6]{0:T(128)S(1)} %dynamic_slice.329) | copy-start | bytes 76
  209.4 102.4 %copy-start.57 = (f32[384]{0:T(512)}, f32[384]{0:T(512)S(1)}, u32[]{:S(2)}) copy-start(f32[384]{0:T(512)S(1)} %dynamic_slice.330) | copy-start | bytes 4612
  321.2 417.9 %all-reduce.15.cloned.1.call-start = ((), (), s32[]{:S(2)}) async-start(), calls=%async_computation.17 | async-start | bytes 2097152 | tf_op jit(solution)/shard_map/psum | solution.py:283
  705.5 99.6 %reduce-scatter.19.cloned.1.call-start = ((), (), s32[]{:S(2)}) async-start(), calls=%async_computation.16 | async-start | bytes 442368
  712.6 132.0 %reduce-scatter.11.cloned.1.call-start = ((), (), s32[]{:S(2)}) async-start(), calls=%async_computation.10 | async-start | bytes 3932160 | tf_op jit(solution)/shard_map/reduce_scatter | solution.py:305
  745.8 11.6 %collective-permute-start.2 = (f32[3,640]{0,1:T(8,128)S(1)}, f32[3,640]{0,1:T(8,128)S(1)}, u32[]{:S(2)}, u32[]{:S(2)}) collective-permute-start(f32[3,640]{0,1:T(8,128)S(1)} %pad_add_fusion.1), channel_id=1, source_target_pairs={{4,0},{8,4},{12,8},{16,12},{20,16},{24,20},{28,24},{5,1},{9,5},{13... | collective-permute-start | bytes 23048 | tf_op jit(solution)/shard_map/ppermute | solution.py:17
  761.9 126.2 %reduce-scatter.9.cloned.1.call-start = ((), (), s32[]{:S(2)}) async-start(), calls=%async_computation.8 | async-start | bytes 3932160 | tf_op jit(solution)/shard_map/reduce_scatter | solution.py:249
  766.3 187.7 %reduce-scatter.17.cloned.1.call-start = ((), (), s32[]{:S(2)}) async-start(), calls=%async_computation.13 | async-start | bytes 1327104 | tf_op jit(solution)/shard_map/reduce_scatter | solution.py:315
  770.5 249.7 %reduce-scatter.15.cloned.1.call-start = ((), (), s32[]{:S(2)}) async-start(), calls=%async_computation.12 | async-start | bytes 884736 | tf_op jit(solution)/shard_map/reduce_scatter | solution.py:313
  772.5 320.3 %reduce-scatter.13.cloned.1.call-start = ((), (), s32[]{:S(2)}) async-start(), calls=%async_computation.11 | async-start | bytes 2654208 | tf_op jit(solution)/shard_map/reduce_scatter | solution.py:312
  777.4 67.2 %copy-start.20 = (f32[256,768]{1,0:T(8,128)S(1)}, f32[256,768]{1,0:T(8,128)}, u32[]{:S(2)}) copy-start(f32[256,768]{1,0:T(8,128)} %param.26) | copy-start | bytes 2359300
  777.4 67.2 %copy-start.25 = (bf16[768,256]{1,0:T(8,128)(2,1)S(1)}, bf16[768,256]{1,0:T(8,128)(2,1)}, u32[]{:S(2)}) copy-start(bf16[768,256]{1,0:T(8,128)(2,1)} %copy-done.24) | copy-start | bytes 1179652
  777.4 67.2 %copy-start.66 = (f32[768]{0:T(1024)S(1)}, f32[768]{0:T(1024)}, u32[]{:S(2)}) copy-start(f32[768]{0:T(1024)} %param.27) | copy-start | bytes 9220
  777.4 67.2 %copy-start.80 = (f32[256]{0:T(256)S(1)}, f32[256]{0:T(256)}, u32[]{:S(2)}) copy-start(f32[256]{0:T(256)} %copy-done.79) | copy-start | bytes 3076
  807.0 81.1 %copy-start.85 = (f32[256]{0:T(256)S(1)}, f32[256]{0:T(256)}, u32[]{:S(2)}) copy-start(f32[256]{0:T(256)} %get-tuple-element.2152) | copy-start | bytes 3076
  888.1 204.6 %copy-start.1 = (f32[4,1536]{1,0:T(4,128)S(1)}, f32[4,1536]{1,0:T(4,128)}, u32[]{:S(2)}) copy-start(f32[4,1536]{1,0:T(4,128)} %param.31) | copy-start | bytes 73732
  (121 other events, 821.6 us)
Sparse Core Ops, SparseCore 0:
  10.3 45.0 all-gather.11
  57.5 18.0 all-gather.9
  205.7 48.2 all-gather.15
  256.0 18.7 all-gather.13
  321.3 41.2 all-gather.17
  705.7 33.3 all-reduce.14
  742.3 62.7 reduce-scatter.18
  807.6 36.8 reduce-scatter.10
  847.1 38.0 reduce-scatter.8
  889.0 64.9 reduce-scatter.16
  957.9 62.3 reduce-scatter.14
  1024.1 68.5 reduce-scatter.12
where the time goes:
time: 1120 us; the launch traced here: 1100 us
  waiting for transfers between devices  302 us (27%)
  local copies, waits for them, and re-layouts  232 us (21%)
  other arithmetic  195 us (17%)
  matrix products  177 us (16%)
  blocking collectives  167 us (15%)
  between operations  15.8 us (1%)
    dynamic_update_slice x44, local copies, waits for them, and re-layouts, ssd_groups(): lax.scan(advance, start_state, (to_blocks(inner_x), to_blocks(state_b), t...  109 us
    another operation x74, other arithmetic  83.4 us
    reduce_scatter x1, waiting for transfers between devices, per_device(): lax.psum_scatter(g_zx, 'dp', scatter_dimension=1, tiled=True)  72.5 us
    reduce_scatter x1, waiting for transfers between devices, per_device(): lax.psum_scatter(g_bc, 'dp', scatter_dimension=0, tiled=True)  66.2 us
    reduce_scatter x1, waiting for transfers between devices, per_device(): lax.psum_scatter(g_out, 'dp', scatter_dimension=1, tiled=True)  62.8 us
    dot_general x12, matrix products, advance(): jnp.einsum('tsh,shp->thp', mixing, weighted_x, precision=exact_prec)  48 us
    psum x1, blocking collectives, per_device(): lax.psum((g_norm_local, place_slice(g_conv_w[:, :inner_here], inner_total...  41 us
    reduce_scatter x1, waiting for transfers between devices, per_device(): lax.psum_scatter(partial_rows, 'tensor', scatter_dimension=0, tiled=True)  37.5 us
  transfers between devices with their start and end apart: 15, of which 8 were waited for; matrix products, arithmetic and copies ran while one was open for 18% of the time, Pallas kernels for 0%

commit v1 on v0

v1 whole, which is shorter than its diff:
```python
import functools
import jax
import jax.numpy as jnp
from jax import lax
from jax.experimental import pallas as pl
from jax.experimental.pallas import tpu as pltpu
from jax.sharding import PartitionSpec as P

GROUP = 256
exact_prec = lax.Precision.HIGHEST
PAD = 8


def dot_wide(left, right):
    return jnp.dot(left, right, preferred_element_type=jnp.float32)


def dot_exact(left, right):
    return jnp.dot(left, right, precision=exact_prec, preferred_element_type=jnp.float32)


def dot_nt(left, right):
    return lax.dot_general(left, right, (((1,), (1,)), ((), ())), preferred_element_type=jnp.float32)


def dot_tn(left, right):
    return lax.dot_general(left, right, (((0,), (0,)), ((), ())), preferred_element_type=jnp.float32)


def head_maps(inner, head_size):
    wide = (
        lax.broadcasted_iota(jnp.int32, (PAD, inner), 1) // head_size
        == lax.broadcasted_iota(jnp.int32, (PAD, inner), 0)
    ).astype(jnp.float32)
    tall = (
        lax.broadcasted_iota(jnp.int32, (inner, PAD), 0) // head_size
        == lax.broadcasted_iota(jnp.int32, (inner, PAD), 1)
    ).astype(jnp.float32)
    return wide, tall


def block_terms(rows, la_ref, lat_ref, key_ref, keyt_ref, before):
    size = rows.size
    row_i = lax.broadcasted_iota(jnp.int32, (size, size), 0)
    col_i = lax.broadcasted_iota(jnp.int32, (size, size), 1)
    lower = row_i >= col_i
    lower_f = lower.astype(jnp.float32)
    upper_f = (row_i <= col_i).astype(jnp.float32)
    la = la_ref[rows, :]
    cum = dot_exact(lower_f, la)
    cumt = dot_exact(lat_ref[:, rows], upper_f)
    key = key_ref[rows, :]
    keyt = keyt_ref[:, rows]
    same = lower & (key == keyt)
    last_key = key[size - 1 :, :]
    last = cum[size - 1 :, :]
    inflow = jnp.where(key == before, jnp.exp(cum), 0.0)
    tail = jnp.where(key == last_key, jnp.exp(last - cum), 0.0)
    passing = jnp.where(last_key == before, jnp.exp(last), 0.0)
    passing_t = jnp.where(last_key == before, jnp.exp(cumt[:, size - 1 :]), 0.0)
    return cum, cumt, same, inflow, tail, passing, passing_t, last_key


def head_decay(same, cum, cumt, head):
    spread = jnp.where(same, cum[:, head : head + 1] - cumt[head : head + 1, :], -1e30)
    return jnp.exp(spread)


def scan_forward_kernel(
    heads, head_size, size, x_ref, b_ref, c_ref, dt_ref, dtt_ref, la_ref, lat_ref, key_ref,
    keyt_ref, before_ref, y_ref, end_ref, inflow_ref,
):
    tokens, inner = x_ref.shape
    wide, tall = head_maps(inner, head_size)
    end_ref[...] = jnp.zeros_like(end_ref)
    first_before = before_ref[...]

    def step(index, carry):
        before, total = carry
        rows = pl.ds(pl.multiple_of(index * size, size), size)
        cum, cumt, same, inflow, tail, passing, passing_t, last_key = block_terms(
            rows, la_ref, lat_ref, key_ref, keyt_ref, before
        )
        x, b, c = x_ref[rows, :], b_ref[rows, :], c_ref[rows, :]
        scores = dot_nt(c, b)
        state = end_ref[...]
        carried = dot_nt(c, state.astype(jnp.bfloat16)) * dot_exact(inflow, wide)
        for head in range(heads):
            cols = slice(head * head_size, (head + 1) * head_size)
            mixing = (
                scores * head_decay(same, cum, cumt, head) * dtt_ref[head : head + 1, rows]
            ).astype(jnp.bfloat16)
            y_ref[rows, cols] = dot_wide(mixing, x[:, cols]) + carried[:, cols]
        pushed = (x.astype(jnp.float32) * dot_exact(tail * dt_ref[rows, :], wide)).astype(
            jnp.bfloat16
        )
        end_ref[...] = state * dot_exact(tall, passing_t) + dot_tn(pushed, b)
        reach = jnp.where(key_ref[rows, :] == first_before, jnp.exp(cum + total), 0.0)
        inflow_ref[rows, :] = dot_exact(reach, wide)
        return last_key, total + cum[size - 1 :, :]

    lax.fori_loop(0, tokens // size, step, (first_before, jnp.zeros((1, PAD), jnp.float32)))


def scan_backward_kernel(
    heads, head_size, size, x_ref, b_ref, c_ref, dy_ref, dt_ref, dtt_ref, la_ref, lat_ref,
    key_ref, keyt_ref, before_ref, skip_ref, entry_ref, exit_ref,
    dx_ref, db_ref, dc_ref, dcum_ref, colt_ref, const_ref, sx_ref, states, cot,
):
    tokens, inner = x_ref.shape
    blocks = tokens // size
    wide, tall = head_maps(inner, head_size)
    states[0] = entry_ref[...]
    first_before = before_ref[...]

    def block_before(index):
        if isinstance(index, int) and index == 0:
            return first_before
        return key_ref[pl.ds(index * size - 1, 1), :]

    def block_rows(index):
        return pl.ds(index * size, size)

    for index in range(blocks - 1):
        rows = block_rows(index)
        terms = block_terms(rows, la_ref, lat_ref, key_ref, keyt_ref, block_before(index))
        tail, passing_t = terms[4], terms[6]
        pushed = (
            x_ref[rows, :].astype(jnp.float32) * dot_exact(tail * dt_ref[rows, :], wide)
        ).astype(jnp.bfloat16)
        states[index + 1] = states[index] * dot_exact(tall, passing_t) + dot_tn(
            pushed, b_ref[rows, :]
        )
    cot[...] = exit_ref[...]

    def step(turn, carry):
        index = blocks - 1 - turn
        rows = pl.ds(pl.multiple_of(index * size, size), size)
        prior = key_ref[pl.ds(jnp.maximum(index * size - 1, 0), 1), :]
        before = jnp.where(index == 0, first_before, prior)
        cum, cumt, same, inflow, tail, passing, passing_t, last_key = block_terms(
            rows, la_ref, lat_ref, key_ref, keyt_ref, before
        )
        strict = lax.broadcasted_iota(jnp.int32, (size, size), 0) > lax.broadcasted_iota(
            jnp.int32, (size, size), 1
        )
        x, b, c = x_ref[rows, :], b_ref[rows, :], c_ref[rows, :]
        x_wide = x.astype(jnp.float32)
        dy = dy_ref[rows, :]
        dy_low = dy.astype(jnp.bfloat16)
        dt = dt_ref[rows, :]
        state, grad = states[index], cot[...]
        state_low, grad_low = state.astype(jnp.bfloat16), grad.astype(jnp.bfloat16)
        scores = dot_nt(c, b)
        from_state = dot_nt(c, state_low)
        from_grad = dot_nt(b, grad_low)
        tail_wide = dot_exact(tail, wide)
        dt_wide = dot_exact(dt, wide)
        d_in = (dy * dot_exact(inflow, wide)).astype(jnp.bfloat16)
        pushed = (x_wide * tail_wide * dt_wide).astype(jnp.bfloat16)
        d_scores = jnp.zeros((size, size), jnp.float32)
        dxd = []
        row_sums = []
        for head in range(heads):
            cols = slice(head * head_size, (head + 1) * head_size)
            decay = head_decay(same, cum, cumt, head)
            mixing = scores * decay
            both = dot_nt(dy_low[:, cols], x[:, cols]) * dtt_ref[head : head + 1, rows]
            d_scores = d_scores + both * decay
            joint = jnp.where(strict, both * mixing, 0.0)
            row_sums.append(jnp.sum(joint, axis=1, keepdims=True))
            colt_ref[head : head + 1, rows] = jnp.sum(joint, axis=0, keepdims=True)
            dxd.append(dot_tn(mixing.astype(jnp.bfloat16), dy_low[:, cols]))
        for head in range(heads, PAD):
            row_sums.append(jnp.zeros((size, 1), jnp.float32))
            colt_ref[head : head + 1, rows] = jnp.zeros((1, size), jnp.float32)
        dxd = jnp.concatenate(dxd, axis=1) + from_grad * tail_wide
        sx_ref[rows, :] = dot_exact(dxd * x_wide, tall)
        dx_ref[rows, :] = dxd * dt_wide + dy * skip_ref[...]
        d_low = d_scores.astype(jnp.bfloat16)
        dc_ref[rows, :] = dot_wide(d_low, b) + dot_wide(d_in, state_low)
        db_ref[rows, :] = dot_tn(d_low, c) + dot_wide(pushed, grad_low)
        through = dot_exact(dy * from_state, tall) * inflow
        kept = dot_exact(x_wide * from_grad, tall) * tail * dt
        dcum_ref[rows, :] = jnp.concatenate(row_sums, axis=1) + through - kept
        whole = dot_exact(jnp.sum(state * grad, axis=1, keepdims=True).T, tall)
        const_ref[rows, :] = jnp.broadcast_to(
            jnp.sum(kept, axis=0, keepdims=True) + passing * whole, (size, PAD)
        )
        cot[...] = grad * dot_exact(tall, passing_t) + dot_tn(d_in, c)
        return carry

    lax.fori_loop(0, blocks, step, 0)


def vmem(count):
    return [pl.BlockSpec(memory_space=pltpu.VMEM)] * count


def scan_forward(x, b, c, dt, dtt, la, lat, key, keyt, before, heads):
    tokens, inner = x.shape
    size = min(GROUP, tokens)
    return pl.pallas_call(
        functools.partial(scan_forward_kernel, heads, inner // heads, size),
        out_shape=(
            jax.ShapeDtypeStruct((tokens, inner), jnp.float32),
            jax.ShapeDtypeStruct((inner, b.shape[1]), jnp.float32),
            jax.ShapeDtypeStruct((tokens, inner), jnp.float32),
        ),
        in_specs=vmem(10),
        out_specs=tuple(vmem(3)),
        compiler_params=pltpu.CompilerParams(vmem_limit_bytes=40 * 2**20),
        name="scan_forward",
    )(x, b, c, dt, dtt, la, lat, key, keyt, before)


def scan_backward(
    x, b, c, dy, dt, dtt, la, lat, key, keyt, before, skip, entry, leave, heads
):
    tokens, inner = x.shape
    size = min(GROUP, tokens)
    wide = b.shape[1]
    return pl.pallas_call(
        functools.partial(scan_backward_kernel, heads, inner // heads, size),
        out_shape=(
            jax.ShapeDtypeStruct((tokens, inner), jnp.float32),
            jax.ShapeDtypeStruct((tokens, wide), jnp.float32),
            jax.ShapeDtypeStruct((tokens, wide), jnp.float32),
            jax.ShapeDtypeStruct((tokens, PAD), jnp.float32),
            jax.ShapeDtypeStruct((PAD, tokens), jnp.float32),
            jax.ShapeDtypeStruct((tokens, PAD), jnp.float32),
            jax.ShapeDtypeStruct((tokens, PAD), jnp.float32),
        ),
        in_specs=vmem(14),
        out_specs=tuple(vmem(7)),
        scratch_shapes=[
            pltpu.VMEM((tokens // size, inner, wide), jnp.float32),
            pltpu.VMEM((inner, wide), jnp.float32),
        ],
        compiler_params=pltpu.CompilerParams(vmem_limit_bytes=48 * 2**20),
        name="scan_backward",
    )(x, b, c, dy, dt, dtt, la, lat, key, keyt, before, skip, entry, leave)


def step_gradients(dcum, colt, const, sx, dt, la, rate):
    tokens = dcum.shape[0]
    size = min(GROUP, tokens)
    change = (dcum - colt.T).reshape(tokens // size, size, PAD)
    index = jnp.arange(size, dtype=jnp.int32)
    upper = (index[:, None] <= index[None, :]).astype(jnp.float32)
    d_la = jnp.einsum("ts,bsh->bth", upper, change, precision=exact_prec).reshape(tokens, PAD)
    d_la = d_la + const
    return d_la * rate + sx, jnp.sum(d_la * la, axis=0)


LENGTH = 4096
EPSILON = 1e-05


def from_behind(block, axis, distance):
    devices = range(lax.axis_size(axis))
    route = [(i - distance, i) for i in devices if i - distance in devices]
    return lax.ppermute(block, axis, route)


def conv_apply(pre_ext, kernel, offsets, validity):
    length = validity.shape[0]
    total = jnp.broadcast_to(offsets[None, :], (length, offsets.shape[0]))
    for offset in range(kernel.shape[0]):
        total = (
            total
            + kernel[offset][None, :]
            * pre_ext[offset : offset + length]
            * validity[:, offset : offset + 1]
        )
    return jax.nn.silu(total)


def place_slice(piece, total_len, start, axis):
    full_shape = list(piece.shape)
    full_shape[axis] = total_len
    return lax.dynamic_update_slice_in_dim(
        jnp.zeros(tuple(full_shape), jnp.float32), piece, start, axis
    )


def pad_to(array, size, axis):
    widths = [(0, 0)] * array.ndim
    widths[axis] = (0, size - array.shape[axis])
    return jnp.pad(array, widths)


def chain(values, decays, mine, backward):
    count = values.shape[0]
    running = jnp.zeros(values.shape[1:], jnp.float32)
    order = range(count - 1, 0, -1) if backward else range(count - 1)
    for index in order:
        longer = running * decays[index] + values[index].astype(jnp.float32)
        reached = index > mine if backward else index < mine
        running = jnp.where(reached, longer, running)
    return running


def per_device(
    block_input,
    norm_gain,
    zx_weight,
    bc_weight,
    dt_weight,
    conv_x_weight,
    conv_x_bias,
    conv_bc_weight,
    conv_bc_bias,
    dt_bias,
    decay_log,
    skip_gain,
    gate_gain,
    out_weight,
    segments,
    cotangent,
):
    low = jnp.bfloat16
    tensor_count = lax.axis_size("tensor")
    tensor_index = lax.axis_index("tensor")
    data_count = lax.axis_size("dp")
    data_index = lax.axis_index("dp")
    token_count = segments.shape[0]
    row_count, width = block_input.shape
    part = zx_weight.shape[1]
    heads_here = dt_weight.shape[1]
    inner_here = out_weight.shape[0]
    head_size = inner_here // heads_here
    inner_total = inner_here * tensor_count
    heads_total = heads_here * tensor_count
    width_back = conv_x_weight.shape[0] - 1
    bc_size = bc_weight.shape[1]
    state_size = bc_size // 2
    head_start = tensor_index * heads_here
    inner_start = tensor_index * inner_here

    def own_heads(array):
        return pad_to(lax.dynamic_slice_in_dim(array, head_start, heads_here), PAD, 0)

    local_bias, local_log, local_skip = map(own_heads, (dt_bias, decay_log, skip_gain))
    local_gate_gain = lax.dynamic_slice_in_dim(gate_gain, inner_start, inner_here)
    skip_wide = jnp.repeat(local_skip[:heads_here], head_size)[None, :]
    conv_weight = jnp.concatenate(
        [lax.dynamic_slice_in_dim(conv_x_weight, inner_start, inner_here, 1), conv_bc_weight],
        axis=1,
    )
    conv_bias = jnp.concatenate(
        [lax.dynamic_slice_in_dim(conv_x_bias, inner_start, inner_here), conv_bc_bias]
    )
    rstd = lax.rsqrt(jnp.mean(block_input * block_input, axis=-1, keepdims=True) + EPSILON)
    normed_rows = (block_input * rstd * norm_gain).astype(low)
    normed = lax.all_gather(normed_rows, "tensor", axis=0, tiled=True)
    extra_size = -(-(bc_size + PAD) // 128) * 128
    side = jnp.concatenate([bc_weight, dt_weight], axis=1)
    side = pad_to(side, max(extra_size, inner_here), 1)
    packed = jnp.stack([zx_weight[0], zx_weight[1], side, out_weight.T])
    every = lax.all_gather(packed, "dp", axis=1, tiled=True)
    w_gate, w_mix, w_side, w_out = every[0], every[1], every[2], every[3]
    cot_full = lax.all_gather(cotangent.astype(low), "tensor", axis=0, tiled=True)

    gate_in = dot_wide(normed, w_gate)
    side_out = dot_wide(normed, w_side)
    pre = jnp.concatenate([dot_wide(normed, w_mix), side_out[:, :bc_size]], axis=1).astype(low)
    raw_dt = side_out[:, bc_size : bc_size + PAD] + local_bias
    step_dt = jax.nn.softplus(raw_dt)
    rate = -jnp.exp(local_log) * (jnp.arange(PAD) < heads_here)
    log_decay = step_dt * rate

    tail_start = token_count - width_back
    own_tail = jnp.concatenate(
        [pre[tail_start:], segments[tail_start:, None].astype(low)], axis=1
    )
    tail = from_behind(own_tail, "dp", 1)
    tail_vals, tail_ids = tail[:, :-1], tail[:, -1].astype(jnp.int32)
    seg_ext = jnp.concatenate([tail_ids, segments])
    pos_ext = (
        data_index * token_count
        - width_back
        + jnp.arange(token_count + width_back, dtype=jnp.int32)
    )
    sequences = data_count * token_count // LENGTH + 1
    key_ext = seg_ext * sequences + pos_ext // LENGTH
    key = key_ext[width_back:]
    before = key_ext[width_back - 1 : width_back].reshape(1, 1)
    validity = jnp.stack(
        [key_ext[k : k + token_count] == key for k in range(width_back + 1)], axis=1
    ).astype(jnp.float32)
    pre_ext = jnp.concatenate([tail_vals, pre], axis=0).astype(jnp.float32)
    activ = conv_apply(pre_ext, conv_weight, conv_bias, validity).astype(low)
    inner_x = activ[:, :inner_here]
    state_b = activ[:, inner_here : inner_here + state_size]
    state_c = activ[:, inner_here + state_size :]
    scan_args = (
        step_dt, step_dt.T, log_decay, log_decay.T, key[:, None], key[None, :], before,
    )
    local_y, local_end, inflow = scan_forward(
        inner_x, state_b, state_c, *scan_args, heads=heads_here
    )

    group = max(1, LENGTH // token_count)
    if data_count % group:
        group = data_count
    lines = [list(range(i, i + group)) for i in range(0, data_count, group)]
    mine = data_index % group

    def gather_line(array):
        return lax.all_gather(array, "dp", axis_index_groups=lines)

    device_decay = jnp.repeat(inflow[-1].reshape(heads_here, head_size)[:, :1], state_size, axis=1)
    sent = jnp.concatenate([local_end.astype(low), pad_to(device_decay, 16, 0).astype(low)])
    arrived = gather_line(sent)
    decays = jnp.repeat(
        arrived[:, inner_here : inner_here + heads_here].astype(jnp.float32), head_size, axis=1
    )
    entry_state = chain(arrived[:, :inner_here], decays, mine, False)
    x_wide = inner_x.astype(jnp.float32)
    mixed = (
        local_y + dot_wide(state_c, entry_state.T.astype(low)) * inflow + skip_wide * x_wide
    )
    sigm = jax.nn.sigmoid(gate_in)
    gate_act = gate_in * sigm
    gated = mixed * gate_act
    d_normed_out = dot_wide(cot_full, w_out)
    scaled = local_gate_gain * d_normed_out
    sums = jnp.stack([jnp.sum(gated * gated, axis=1), jnp.sum(scaled * gated, axis=1)])
    sums = lax.psum(sums, "tensor") / inner_total
    rstd_gate = lax.rsqrt(sums[0] + EPSILON)[:, None]
    gate_dots = sums[1][:, None]
    gated_normed = gated * rstd_gate
    normed_out = (gated_normed * local_gate_gain).astype(low)
    d_gated = rstd_gate * scaled - gated * rstd_gate**3 * gate_dots
    d_mixed = d_gated * gate_act
    state_cot = dot_wide((d_mixed * inflow).T.astype(low), state_c)
    cots = gather_line(state_cot.astype(low))
    leave_cot = chain(cots, decays, mine, True)
    branch = lax.psum_scatter(
        dot_wide(normed_out, w_out.T).astype(low), "tensor", scatter_dimension=0, tiled=True
    )
    result = block_input + branch.astype(jnp.float32)
    g_out = dot_wide(cot_full.T, normed_out).astype(low)
    g_out = lax.psum_scatter(g_out, "dp", scatter_dimension=0, tiled=True)
    g_gate_local = jnp.sum(d_normed_out * gated_normed, axis=0)
    d_gate_in = (d_gated * mixed * sigm * (1.0 + gate_in * (1.0 - sigm))).astype(low)
    g_skip_wide = jnp.sum(d_mixed * x_wide, axis=0)
    g_skip_local = jnp.sum(g_skip_wide.reshape(heads_here, head_size), axis=1)

    d_x, d_b, d_c, dcum, colt, const, sx = scan_backward(
        inner_x, state_b, state_c, d_mixed, *scan_args, skip_wide, entry_state, leave_cot,
        heads=heads_here,
    )
    d_bc = lax.psum(jnp.concatenate([d_b, d_c], axis=1).astype(low), "tensor")
    d_step, d_log = step_gradients(dcum, colt, const, sx, step_dt, log_decay, rate)
    d_activ = jnp.concatenate([d_x, d_bc.astype(jnp.float32)], axis=1)

    def conv_part(values, kernel, offsets):
        return conv_apply(values, kernel, offsets, validity)

    conv_out, conv_back = jax.vjp(conv_part, pre_ext, conv_weight, conv_bias)
    d_pre_ext, g_conv_w, g_conv_b = conv_back(d_activ)
    from_next = from_behind(d_pre_ext[:width_back], "dp", -1)
    d_pre_own = d_pre_ext[width_back:]
    d_pre = jnp.concatenate(
        [d_pre_own[:tail_start], d_pre_own[tail_start:] + from_next], axis=0
    ).astype(low)
    d_raw = d_step * jax.nn.sigmoid(raw_dt)
    g_dt_bias_local = jnp.sum(d_raw, axis=0)
    d_raw_b = d_raw.astype(low)
    d_mix = d_pre[:, :inner_here]
    d_side = jnp.concatenate([d_pre[:, inner_here:], d_raw_b], axis=1)
    partial_rows = (
        dot_wide(d_gate_in, w_gate.T)
        + dot_wide(d_mix, w_mix.T)
        + dot_wide(d_raw_b, w_side[:, bc_size : bc_size + PAD].T)
    )
    own_bc = lax.dynamic_slice_in_dim(d_pre[:, inner_here:], tensor_index * row_count, row_count, 0)
    d_normed_rows = lax.psum_scatter(
        partial_rows.astype(low), "tensor", scatter_dimension=0, tiled=True
    ).astype(jnp.float32) + dot_wide(own_bc, w_side[:, :bc_size].T)
    g_in = jnp.stack(
        [
            dot_wide(normed.T, d_gate_in),
            dot_wide(normed.T, d_mix),
            pad_to(dot_wide(normed.T, d_side), inner_here, 1),
        ]
    ).astype(low)
    g_in = lax.psum_scatter(g_in, "dp", scatter_dimension=1, tiled=True).astype(jnp.float32)
    grad_zx = g_in[:2]
    grad_bc = g_in[2, :, :bc_size]
    grad_dt = g_in[2, :, bc_size : bc_size + heads_here]
    grad_out = g_out.astype(jnp.float32).T
    scaled_in = norm_gain * d_normed_rows
    g_norm_local = jnp.sum(d_normed_rows * block_input * rstd, axis=0)
    grad_input = (
        cotangent
        + rstd * scaled_in
        - block_input * rstd**3 * jnp.mean(scaled_in * block_input, axis=-1, keepdims=True)
    )
    pieces = (
        g_norm_local,
        place_slice(g_conv_w[:, :inner_here], inner_total, inner_start, 1),
        place_slice(g_conv_b[:inner_here], inner_total, inner_start, 0),
        g_conv_w[:, inner_here:] / tensor_count,
        g_conv_b[inner_here:] / tensor_count,
        place_slice(g_dt_bias_local[:heads_here], heads_total, head_start, 0),
        place_slice(d_log[:heads_here], heads_total, head_start, 0),
        place_slice(g_skip_local, heads_total, head_start, 0),
        place_slice(g_gate_local, inner_total, inner_start, 0),
    )
    flat = jnp.concatenate([piece.reshape(-1) for piece in pieces])
    flat = pad_to(flat, -(-flat.shape[0] // 1024) * 1024, 0)
    flat = lax.psum(flat, ("dp", "tensor"))
    small, at = [], 0
    for piece in pieces:
        small.append(flat[at : at + piece.size].reshape(piece.shape))
        at += piece.size
    grad_norm, grad_cxw, grad_cxb, grad_cbw, grad_cbb, grad_dtb, grad_log, grad_skip, grad_gate = (
        small
    )
    return (
        result,
        grad_input,
        grad_norm,
        grad_zx,
        grad_bc,
        grad_dt,
        grad_cxw,
        grad_cxb,
        grad_cbw,
        grad_cbb,
        grad_dtb,
        grad_log,
        grad_skip,
        grad_gate,
        grad_out,
    )


def solution(mesh):
    in_specs = (
        P(("dp", "tensor"), None),
        P(),
        P(None, "dp", "tensor"),
        P("dp", None),
        P("dp", "tensor"),
        P(),
        P(),
        P(),
        P(),
        P(),
        P(),
        P(),
        P(),
        P("tensor", "dp"),
        P("dp"),
        P(("dp", "tensor"), None),
    )
    out_specs = (
        P(("dp", "tensor"), None),
        P(("dp", "tensor"), None),
        P(),
        P(None, "dp", "tensor"),
        P("dp", None),
        P("dp", "tensor"),
        P(),
        P(),
        P(),
        P(),
        P(),
        P(),
        P(),
        P(),
        P("tensor", "dp"),
    )
    return jax.shard_map(
        per_device, mesh=mesh, in_specs=in_specs, out_specs=out_specs, check_vma=False
    )
```

time: 1120 us -> 435 us (0.39); the launches traced: 1100 us -> 434 us
  local copies, waits for them, and re-layouts: 232 us -> 38.1 us
  other arithmetic: 195 us -> 32.3 us
  matrix products: 177 us -> 40.6 us
  waiting for transfers between devices: 302 us -> 200 us
  blocking collectives: 167 us -> 72 us
  Pallas kernels: 0 us -> 31.3 us
    reduce_scatter x5 -> x2, waiting for transfers between devices: 239 us -> 27.7 us  [the longest x1 27.7 us: per_device(): lax.psum_scatter(partial_rows.astype(low), 'tensor', scatter_dimension=0,...]
    dot_general x63 -> x1, matrix products: 142 us -> 0.28 us  [step_gradients(): jnp.einsum('ts,bsh->bth', upper, change, precision=exact_prec)]
    dynamic_update_slice x44 -> x0, local copies, waits for them, and re-layouts: 109 us -> none  [ssd_groups(): lax.scan(advance, start_state, (to_blocks(inner_x), to_blocks(state_b), t...]
    all_gather x4 -> x2, blocking collectives: 115 us -> 26.6 us  [gather_line(): return lax.all_gather(array, 'dp', axis_index_groups=lines)]
    another operation x75 -> x9, other arithmetic: 85 us -> 1.06 us  [the longest x2 0.77 us: per_device(): packed = jnp.stack([zx_weight[0], zx_weight[1], side, out_weight.T])]
    all_gather x4 -> x2, waiting for transfers between devices: 0.04 us -> 54.6 us  [the longest x1 54.6 us: per_device(): every = lax.all_gather(packed, 'dp', axis=1, tiled=True)]
    unnamed x13 -> x10, waiting for transfers between devices: 26.9 us -> 76.4 us
    another operation x91 -> x12, local copies, waits for them, and re-layouts: 36.3 us -> 0.31 us  [the longest x4 0.1 us: per_device(): jnp.stack([key_ext[k:k + token_count] == key for k in range(width_back +...]
  transfers between devices with their start and end apart: 15 -> 10, of which waited for: 8 -> 7; matrix products, arithmetic and copies ran while one was open for 18% -> 18% of each run, Pallas kernels for 0% -> 2%
where the time goes in v1:
time: 435 us; the launch traced here: 434 us
  waiting for transfers between devices  200 us (46%)
  blocking collectives  72 us (17%)
  matrix products  40.6 us (9%)
  local copies, waits for them, and re-layouts  38.1 us (9%)
  other arithmetic  32.3 us (7%)
  Pallas kernels  31.3 us (7%)
  between operations  15.1 us (3%)
    unnamed x10, waiting for transfers between devices  76.4 us
    all_gather x1, waiting for transfers between devices, per_device(): every = lax.all_gather(packed, 'dp', axis=1, tiled=True)  54.6 us
    dot_general x15, matrix products, dot_wide(): return jnp.dot(left, right, preferred_element_type=jnp.float32)  40.3 us
    psum x1, blocking collectives, per_device(): flat = lax.psum(flat, ('dp', 'tensor'))  39.7 us
    reduce_scatter x1, waiting for transfers between devices, per_device(): lax.psum_scatter(partial_rows.astype(low), 'tensor', scatter_dimension=0,...  27.7 us
    all_gather x2, blocking collectives, gather_line(): return lax.all_gather(array, 'dp', axis_index_groups=lines)  26.6 us
    unnamed x143, local copies, waits for them, and re-layouts  25.3 us
    pallas_call x1, Pallas kernels, scan_backward(): pl.pallas_call(functools.partial(scan_backward_kernel, heads, inner // he...  21.5 us
  transfers between devices with their start and end apart: 10, of which 7 were waited for; matrix products, arithmetic and copies ran while one was open for 18% of the time, Pallas kernels for 2%

profile of v1, /device:TPU:0, one launch (start us, length us, event | category | flops | bytes accessed | tf_op | source)
XLA Modules:
  0.0 434.0 jit_solution(13194530116209692951)
XLA Ops:
  15.7 18.1 %all-gather.6.cloned.1.call-done = bf16[1024,768]{1,0:T(8,128)(2,1)} async-done(((bf16[256,768]{1,0:T(8,128)(2,1)}), bf16[1024,768]{1,0:T(8,128)(2,1)}) %all-gather.6.cloned.1.call-update) | async-done | bytes 1572880 | tf_op jit(solution)/shard_map/all_gather | solution.py:356
  33.9 54.6 %all-gather.8.cloned.1.call-done = bf16[4,768,384]{2,1,0:T(8,128)(2,1)} async-done(((bf16[4,96,384]{2,1,0:T(8,128)(2,1)}), bf16[4,768,384]{2,1,0:T(8,128)(2,1)}) %all-gather.8.cloned.1.call-update) | async-done | bytes 2359312 | tf_op jit(solution)/shard_map/all_gather | solution.py:361
  88.5 2.4 fusion.67
  92.3 2.7 convolution_convert_fusion.1
  95.0 2.5 collective-permute-start
  97.5 2.1 fusion.15
  103.1 3.8 multiply_convert_fusion
  109.5 9.8 %scan_forward.1 = (f32[1024,384]{1,0:T(8,128)S(1)}, f32[384,128]{1,0:T(8,128)S(1)}, f32[1024,384]{1,0:T(8,128)S(1)}) custom-call(bf16[1024,384]{1,0:T(8,128)(2,1)S(1)} %slice.371.x_ref, bf16[1024,128]{1,0:T(8,128)(2,1)S(1)} %get-tuple-element.155.b_ref, bf16[1024,128]{1,0:T(8,128)(2,1)S(1)} %get-tuple-element.154.c_ref, f32[1024,8]{1,0:T(8,128)S(1)} %copy.130.dt_ref, ...), custom_call_target="tpu_custom_call" | custom-call | tf_op jit(solution)/shard_map/scan_forward/pallas_call | solution.py:203
  122.3 13.3 %all-gather = bf16[1600,128]{1,0:T(8,128)(2,1)S(1)} all-gather(bf16[400,128]{1,0:T(8,128)(2,1)S(1)} %pad_maximum_fusion.5), channel_id=2, replica_groups={{0,4,8,12},{16,20,24,28},{1,5,9,13},{17,21,25,29},{2,6,10,14},{18,22,26..., dimensions={0}, use_global_device_ids=true | all-gather | bytes 512000 | tf_op jit(solution)/shard_map/all_gather | solution.py:411
  135.7 3.4 fusion.2
  139.8 5.3 %multiply_reduce_fusion.5 = (f32[1024]{0:T(1024)S(1)}, f32[1024]{0:T(1024)S(1)}, f32[1024,384]{1,0:T(8,128)}, f32[384,1024]{0,1:T(8,128)}) fusion(f32[384]{0:T(512)S(1)} %dynamic_slice.26, f32[1024,384]{1,0:T(8,128)} %fusion.2, f32[1024,384]{1,0:T(8,128)} %fusion.15, bf16[1024,768]{1,0:T(8,128)(2,1)} %all-gather.10.cloned.1.call-done, ...), kind=kOutput, calls=%fused_computation.32 | convolution fusion | flops 607909888 | bytes 8463872 | tf_op jit(solution)/shard_map/dot_general | solution.py:15
  145.1 5.8 %psum.21 = f32[2,1024]{1,0:T(2,128)S(1)} all-reduce(f32[2,1024]{1,0:T(2,128)S(1)} %pad_maximum_fusion.6), channel_id=1, replica_groups=mesh['dp'=8,'tensor'=4] {'tensor'}, use_global_device_ids=true, to_apply=%region_3.4 | all-reduce | flops 2048 | bytes 16384 | tf_op jit(solution)/shard_map/psum | solution.py:430
  150.9 5.0 %fusion.3 = (f32[384]{0:T(512)}, f32[1024,384]{1,0:T(8,128)S(1)}, bf16[1024,384]{1,0:T(8,128)(2,1)}, f32[384]{0:T(512)}) fusion(bf16[1024,640]{1,0:T(8,128)(2,1)} %copy-done.17, f32[1024,384]{1,0:T(8,128)} %fusion.15, f32[1024]{0:T(1024)S(1)} %bitcast.187, f32[1024,384]{1,0:T(8,128)} %get-tuple-element.143, f32[1024]{0:T(1024)S(1)} %multiply_multiply_fusion.4, ...), kind=kLoop, calls=%fused_computation.23 | loop fusion | flops 9043200 | bytes 9454080 | tf_op jit(solution)/shard_map/reduce_sum | solution.py:448
  157.7 13.3 %all-gather.1 = bf16[1536,128]{1,0:T(8,128)(2,1)S(1)} all-gather(bf16[384,128]{1,0:T(8,128)(2,1)S(1)} %convolution_convert_fusion.6), channel_id=3, replica_groups={{0,4,8,12},{16,20,24,28},{1,5,9,13},{17,21,25,29},{2,6,10,14},{18,22,26..., dimensions={0}, use_global_device_ids=true | all-gather | bytes 491520 | tf_op jit(solution)/shard_map/all_gather | solution.py:411
  171.1 21.5 %scan_backward.1 = (f32[1024,384]{1,0:T(8,128)}, f32[1024,128]{1,0:T(8,128)S(1)}, f32[1024,128]{1,0:T(8,128)S(1)}, f32[1024,8]{1,0:T(8,128)S(1)}, f32[8,1024]{1,...) custom-call(bf16[1024,384]{1,0:T(8,128)(2,1)S(1)} %slice.371.x_ref, bf16[1024,128]{1,0:T(8,128)(2,1)S(1)} %copy-done.7, ...), custom_call_target="tpu_custom_call" | custom-call | tf_op jit(solution)/shard_map/scan_backward/pallas_call | solution.py:223
  194.5 2.4 fusion.8
  199.5 3.3 fusion.30
  202.8 3.9 fusion.14
  206.7 20.4 %all-reduce.16.cloned.1.call-done = bf16[1024,256]{1,0:T(8,128)(2,1)} async-done(((bf16[1024,256]{1,0:T(8,128)(2,1)}), bf16[1024,256]{1,0:T(8,128)(2,1)}) %all-reduce.16.cloned.1.call-update) | async-done | bytes 524304 | tf_op jit(solution)/shard_map/psum | solution.py:455
  228.7 5.2 %multiply_reduce_fusion.3 = (f32[640]{0:T(1024)S(1)}, f32[640]{0:T(1024)S(1)}, f32[640]{0:T(1024)S(1)}, f32[640]{0:T(1024)S(1)}, f32[640]{0:T(1024)}, /*index=5*/f32[1024,640]{1,0:T(8,128)S(1)}) fusion(f32[1027,640]{1,0:T(8,128)S(1)} %copy-done.12, f32[1024]{0:T(1024)S(1)} %bitcast.177, f32[1024]{0:T(1024)S(1)} %bitcast.180, f32[1024]{0:T(1024)S(1)} %bitcast.183, ...), kind=kLoop, calls=%fused_computation.10 | loop fusion | flops 15070080 | bytes 18379264 | tf_op jit(solution)/shard_map/transpose(jvp())/reduce_sum | solution.py:272
  237.7 2.8 collective-permute-done.1
  243.4 3.3 add_convert_fusion
  248.1 3.3 convolution_convert_fusion
  252.5 2.2 fusion.6
  257.9 3.3 copy.151
  261.3 3.2 copy.158
  267.4 25.8 %reduce-scatter.15.cloned.1.call-done = bf16[96,384]{1,0:T(8,128)(2,1)} async-done(((bf16[768,384]{1,0:T(8,128)(2,1)}), bf16[96,384]{1,0:T(8,128)(2,1)}) %reduce-scatter.15.cloned.1.call-update) | async-done | bytes 73744
  295.0 27.7 %reduce-scatter.11.cloned.1.call-done = bf16[256,768]{1,0:T(8,128)(2,1)} async-done(((bf16[1024,768]{1,0:T(8,128)(2,1)}), bf16[256,768]{1,0:T(8,128)(2,1)}) %reduce-scatter.11.cloned.1.call-update) | async-done | bytes 393232 | tf_op jit(solution)/shard_map/reduce_scatter | solution.py:480
  322.7 2.9 multiply_reduce_fusion.6
  326.3 39.7 %psum.23 = f32[12288]{0:T(1024)S(1)} all-reduce(f32[12288]{0:T(1024)S(1)} %pad.64), channel_id=1, replica_groups=mesh['dp'=8,'tensor'=4] {'dp','tensor'}, use_global_device_ids=true, to_apply=%region_19.20 | all-reduce | flops 12288 | bytes 98304 | tf_op jit(solution)/shard_map/psum | solution.py:515
  370.4 2.7 multiply_subtract_fusion.1
  373.1 50.4 %reduce-scatter.13.cloned.1.call-done = bf16[96,1152]{1,0:T(8,128)(2,1)} async-done(((bf16[768,1152]{1,0:T(8,128)(2,1)}), bf16[96,1152]{1,0:T(8,128)(2,1)}) %reduce-scatter.13.cloned.1.call-update) | async-done | bytes 221200
  (280 shorter events, 52.7 us)
Async XLA Ops:
  7.2 6.6 %copy-start = (f32[4,1536]{1,0:T(4,128)S(1)}, f32[4,1536]{1,0:T(4,128)}, u32[]{:S(2)}) copy-start(f32[4,1536]{1,0:T(4,128)} %param.21) | copy-start | bytes 73732
  7.2 26.6 %all-gather.6.cloned.1.call-start = ((), (), s32[]{:S(2)}) async-start(), calls=%async_computation.4 | async-start | bytes 1966080 | tf_op jit(solution)/shard_map/all_gather | solution.py:356
  11.3 77.1 %all-gather.8.cloned.1.call-start = ((), (), s32[]{:S(2)}) async-start(), calls=%async_computation.5 | async-start | bytes 2654208 | tf_op jit(solution)/shard_map/all_gather | solution.py:361
  12.4 127.4 %all-gather.10.cloned.1.call-start = ((), (), s32[]{:S(2)}) async-start(), calls=%async_computation.6 | async-start | bytes 1966080 | tf_op jit(solution)/shard_map/all_gather | solution.py:363
  13.2 213.9 %all-reduce.16.cloned.1.call-start = ((), (), s32[]{:S(2)}) async-start(), calls=%async_computation.8 | async-start | bytes 1048576 | tf_op jit(solution)/shard_map/psum | solution.py:455
  14.8 85.7 %copy-start.49 = (f32[8]{0:T(128)}, f32[8]{0:T(128)S(1)}, u32[]{:S(2)}) copy-start(f32[8]{0:T(128)S(1)} %compare_select_fusion.1) | copy-start | bytes 100
  15.5 135.4 %copy-start.39 = (f32[384]{0:T(512)}, f32[384]{0:T(512)S(1)}, u32[]{:S(2)}) copy-start(f32[384]{0:T(512)S(1)} %dynamic_slice.26) | copy-start | bytes 4612
  15.7 87.5 %copy-start.34 = (f32[640]{0:T(1024)}, f32[640]{0:T(1024)S(1)}, u32[]{:S(2)}) copy-start(f32[640]{0:T(1024)S(1)} %get-tuple-element.136) | copy-start | bytes 7684
  15.7 87.5 %copy-start.36 = (f32[640]{0:T(1024)}, f32[640]{0:T(1024)S(1)}, u32[]{:S(2)}) copy-start(f32[640]{0:T(1024)S(1)} %get-tuple-element.137) | copy-start | bytes 7684
  15.7 84.8 %copy-start.51 = (f32[8]{0:T(128)}, f32[8]{0:T(128)S(1)}, u32[]{:S(2)}) copy-start(f32[8]{0:T(128)S(1)} %pad.52) | copy-start | bytes 100
  92.3 5.2 %copy-start.20 = (bf16[4,768,384]{2,1,0:T(8,128)(2,1)S(1)}, bf16[4,768,384]{2,1,0:T(8,128)(2,1)}, u32[]{:S(2)}) copy-start(bf16[4,768,384]{2,1,0:T(8,128)(2,1)} %all-gather.8.cloned.1.call-done) | copy-start | bytes 7077892
  95.0 6.8 %collective-permute-start = (bf16[3,641]{1,0:T(4,128)(2,1)S(1)}, bf16[3,641]{1,0:T(4,128)(2,1)S(1)}, u32[]{:S(2)}, u32[]{:S(2)}) collective-permute-start(bf16[3,641]{1,0:T(4,128)(2,1)S(1)} %fusion.48), channel_id=1, source_target_pairs={{0,4},{4,8},{8,12},{12,16},{16,20},{20,24},{24,28},{1,5},{5,9},{9,... | collective-permute-start | bytes 11546 | tf_op jit(solution)/shard_map/ppermute | solution.py:263
  108.2 12.9 %copy-start.4 = (bf16[1024,128]{1,0:T(8,128)(2,1)}, bf16[1024,128]{1,0:T(8,128)(2,1)S(1)}, u32[]{:S(2)}) copy-start(bf16[1024,128]{1,0:T(8,128)(2,1)S(1)} %get-tuple-element.154.c_ref) | copy-start | bytes 786436
  108.2 12.9 %copy-start.6 = (bf16[1024,128]{1,0:T(8,128)(2,1)}, bf16[1024,128]{1,0:T(8,128)(2,1)S(1)}, u32[]{:S(2)}) copy-start(bf16[1024,128]{1,0:T(8,128)(2,1)S(1)} %get-tuple-element.155.b_ref) | copy-start | bytes 786436
  156.0 15.1 %copy-start.3 = (s32[1024,1]{1,0:T(8,128)S(1)}, s32[1024,1]{1,0:T(8,128)}, u32[]{:S(2)}) copy-start(s32[1024,1]{1,0:T(8,128)} %copy.132.key_ref) | copy-start | bytes 12292
  156.0 15.1 %copy-start.5 = (bf16[1024,128]{1,0:T(8,128)(2,1)S(1)}, bf16[1024,128]{1,0:T(8,128)(2,1)}, u32[]{:S(2)}) copy-start(bf16[1024,128]{1,0:T(8,128)(2,1)} %copy-done.4) | copy-start | bytes 786436
  156.0 15.1 %copy-start.7 = (bf16[1024,128]{1,0:T(8,128)(2,1)S(1)}, bf16[1024,128]{1,0:T(8,128)(2,1)}, u32[]{:S(2)}) copy-start(bf16[1024,128]{1,0:T(8,128)(2,1)} %copy-done.6) | copy-start | bytes 786436
  156.0 15.1 %copy-start.9 = (f32[384,128]{1,0:T(8,128)S(1)}, f32[384,128]{1,0:T(8,128)}, u32[]{:S(2)}) copy-start(f32[384,128]{1,0:T(8,128)} %copy-done.8) | copy-start | bytes 589828
  193.6 99.6 %reduce-scatter.15.cloned.1.call-start = ((), (), s32[]{:S(2)}) async-start(), calls=%async_computation.11 | async-start | bytes 663552
  202.7 120.0 %reduce-scatter.11.cloned.1.call-start = ((), (), s32[]{:S(2)}) async-start(), calls=%async_computation.9 | async-start | bytes 1966080 | tf_op jit(solution)/shard_map/reduce_scatter | solution.py:480
  202.8 25.6 %copy-start.12 = (f32[1027,640]{1,0:T(8,128)S(1)}, f32[1027,640]{1,0:T(8,128)}, u32[]{:S(2)}) copy-start(f32[1027,640]{1,0:T(8,128)} %copy-done.11) | copy-start | bytes 7887364
  234.9 5.6 %collective-permute-start.1 = (f32[3,640]{1,0:T(4,128)S(1)}, f32[3,640]{1,0:T(4,128)S(1)}, u32[]{:S(2)}, u32[]{:S(2)}) collective-permute-start(f32[3,640]{1,0:T(4,128)S(1)} %pad_add_fusion.1), channel_id=1, source_target_pairs={{4,0},{8,4},{12,8},{16,12},{20,16},{24,20},{28,24},{5,1},{9,5},{13... | collective-permute-start | bytes 23048 | tf_op jit(solution)/shard_map/ppermute | solution.py:263
  246.7 123.7 %reduce-scatter.9.cloned.1.call-start = ((), (), s32[]{:S(2)}) async-start(), calls=%async_computation.7 | async-start | bytes 1966080 | tf_op jit(solution)/shard_map/reduce_scatter | solution.py:440
  251.4 172.1 %reduce-scatter.13.cloned.1.call-start = ((), (), s32[]{:S(2)}) async-start(), calls=%async_computation.10 | async-start | bytes 1990656
  264.5 58.2 %copy-start.14 = (f32[256,768]{1,0:T(8,128)S(1)}, f32[256,768]{1,0:T(8,128)}, u32[]{:S(2)}) copy-start(f32[256,768]{1,0:T(8,128)} %param.16) | copy-start | bytes 2359300
  264.5 58.2 %copy-start.26 = (bf16[768,384]{1,0:T(8,128)(2,1)S(1)}, bf16[768,384]{1,0:T(8,128)(2,1)}, u32[]{:S(2)}) copy-start(bf16[768,384]{1,0:T(8,128)(2,1)} %slice_bitcast_fusion.2) | copy-start | bytes 1769476
  264.5 58.2 %copy-start.33 = (f32[768]{0:T(1024)S(1)}, f32[768]{0:T(1024)}, u32[]{:S(2)}) copy-start(f32[768]{0:T(1024)} %param.17) | copy-start | bytes 9220
  264.5 58.2 %copy-start.44 = (f32[256]{0:T(256)S(1)}, f32[256]{0:T(256)}, u32[]{:S(2)}) copy-start(f32[256]{0:T(256)} %copy-done.43) | copy-start | bytes 3076
  295.0 30.6 %copy-start.58 = (f32[24]{0:T(128)S(1)}, f32[24]{0:T(128)}, u32[]{:S(2)}) copy-start(f32[24]{0:T(128)} %copy-done.57) | copy-start | bytes 292
  295.0 30.6 %copy-start.60 = (f32[24]{0:T(128)S(1)}, f32[24]{0:T(128)}, u32[]{:S(2)}) copy-start(f32[24]{0:T(128)} %copy-done.59) | copy-start | bytes 292
  295.0 75.4 %copy-start.22 = (f32[256,768]{1,0:T(8,128)S(1)}, f32[256,768]{1,0:T(8,128)}, u32[]{:S(2)}) copy-start(f32[256,768]{1,0:T(8,128)} %param.31) | copy-start | bytes 2359300
  295.0 75.4 %copy-start.47 = (f32[256]{0:T(256)S(1)}, f32[256]{0:T(256)}, u32[]{:S(2)}) copy-start(f32[256]{0:T(256)} %get-tuple-element.177) | copy-start | bytes 3076
  (43 other events, 107.7 us)
Sparse Core Ops, SparseCore 0:
  11.5 22.3 all-gather.5
  36.6 51.8 all-gather.7
  90.0 18.1 all-gather.9
  193.7 33.3 all-reduce.15
  230.3 62.8 reduce-scatter.14
  295.6 27.0 reduce-scatter.10
  325.2 27.9 reduce-scatter.8
  356.7 66.7 reduce-scatter.12

commit v2 on v1

--- a/solution.py
+++ b/solution.py
@@ -5,6 +5,7 @@
 from jax.experimental import pallas as pl
 from jax.experimental.pallas import tpu as pltpu
 from jax.sharding import PartitionSpec as P
+
 
 GROUP = 256
 exact_prec = lax.Precision.HIGHEST
@@ -78,7 +79,7 @@
     def step(index, carry):
         before, total = carry
         rows = pl.ds(pl.multiple_of(index * size, size), size)
-        cum, cumt, same, inflow, tail, passing, passing_t, last_key = block_terms(
+        cum, cumt, same, inflow, tail, _, passing_t, last_key = block_terms(
             rows, la_ref, lat_ref, key_ref, keyt_ref, before
         )
         x, b, c = x_ref[rows, :], b_ref[rows, :], c_ref[rows, :]
@@ -138,7 +139,7 @@
         rows = pl.ds(pl.multiple_of(index * size, size), size)
         prior = key_ref[pl.ds(jnp.maximum(index * size - 1, 0), 1), :]
         before = jnp.where(index == 0, first_before, prior)
-        cum, cumt, same, inflow, tail, passing, passing_t, last_key = block_terms(
+        cum, cumt, same, inflow, tail, passing, passing_t, _ = block_terms(
             rows, la_ref, lat_ref, key_ref, keyt_ref, before
         )
         strict = lax.broadcasted_iota(jnp.int32, (size, size), 0) > lax.broadcasted_iota(
@@ -242,7 +243,7 @@
     )(x, b, c, dy, dt, dtt, la, lat, key, keyt, before, skip, entry, leave)
 
 
-def step_gradients(dcum, colt, const, sx, dt, la, rate):
+def step_gradients(dcum, colt, const, sx, la, rate):
     tokens = dcum.shape[0]
     size = min(GROUP, tokens)
     change = (dcum - colt.T).reshape(tokens // size, size, PAD)
@@ -251,6 +252,50 @@
     d_la = jnp.einsum("ts,bsh->bth", upper, change, precision=exact_prec).reshape(tokens, PAD)
     d_la = d_la + const
     return d_la * rate + sx, jnp.sum(d_la * la, axis=0)
+
+
+def spread_kernel(axis, group, own_ref, out_ref, send_sem, recv_sem):
+    place = lax.axis_index(axis)
+    mine = lax.rem(place, group)
+    base = place - mine
+    barrier = pltpu.get_barrier_semaphore()
+    peers = [base + lax.rem(mine + k, group) for k in range(1, group)]
+    for peer in peers:
+        pl.semaphore_signal(
+            barrier, inc=1, device_id={axis: peer}, device_id_type=pl.DeviceIdType.MESH
+        )
+    pl.semaphore_wait(barrier, group - 1)
+    copies = []
+    for k, peer in enumerate(peers):
+        copy = pltpu.make_async_remote_copy(
+            src_ref=own_ref,
+            dst_ref=out_ref.at[mine],
+            send_sem=send_sem.at[k],
+            recv_sem=recv_sem.at[k],
+            device_id={axis: peer},
+            device_id_type=pl.DeviceIdType.MESH,
+        )
+        copy.start()
+        copies.append(copy)
+    out_ref[mine] = own_ref[...]
+    for copy in copies:
+        copy.wait()
+
+
+def spread(array, axis, group, number):
+    if group == 1:
+        return array[None]
+    return pl.pallas_call(
+        functools.partial(spread_kernel, axis, group),
+        out_shape=jax.ShapeDtypeStruct((group,) + array.shape, array.dtype),
+        in_specs=vmem(1),
+        out_specs=vmem(1)[0],
+        scratch_shapes=[
+            pltpu.SemaphoreType.DMA((group - 1,)),
+            pltpu.SemaphoreType.DMA((group - 1,)),
+        ],
+        compiler_params=pltpu.CompilerParams(collective_id=number, has_side_effects=True),
+    )(array)
 
 
 LENGTH = 4096
@@ -274,14 +319,6 @@
             * validity[:, offset : offset + 1]
         )
     return jax.nn.silu(total)
-
-
-def place_slice(piece, total_len, start, axis):
-    full_shape = list(piece.shape)
-    full_shape[axis] = total_len
-    return lax.dynamic_update_slice_in_dim(
-        jnp.zeros(tuple(full_shape), jnp.float32), piece, start, axis
-    )
 
 
 def pad_to(array, size, axis):
@@ -325,13 +362,11 @@
     data_count = lax.axis_size("dp")
     data_index = lax.axis_index("dp")
     token_count = segments.shape[0]
-    row_count, width = block_input.shape
-    part = zx_weight.shape[1]
+    row_count, _ = block_input.shape
     heads_here = dt_weight.shape[1]
     inner_here = out_weight.shape[0]
     head_size = inner_here // heads_here
     inner_total = inner_here * tensor_count
-    heads_total = heads_here * tensor_count
     width_back = conv_x_weight.shape[0] - 1
     bc_size = bc_weight.shape[1]
     state_size = bc_size // 2
@@ -357,10 +392,14 @@
     extra_size = -(-(bc_size + PAD) // 128) * 128
     side = jnp.concatenate([bc_weight, dt_weight], axis=1)
     side = pad_to(side, max(extra_size, inner_here), 1)
-    packed = jnp.stack([zx_weight[0], zx_weight[1], side, out_weight.T])
+    packed = jnp.concatenate([zx_weight, side[None]])
     every = lax.all_gather(packed, "dp", axis=1, tiled=True)
-    w_gate, w_mix, w_side, w_out = every[0], every[1], every[2], every[3]
-    cot_full = lax.all_gather(cotangent.astype(low), "tensor", axis=0, tiled=True)
+    out_part, cot_rows, every, normed = lax.optimization_barrier(
+        (out_weight.T, cotangent.astype(low), every, normed)
+    )
+    w_gate, w_mix, w_side = every[0], every[1], every[2]
+    w_out = lax.all_gather(out_part, "dp", axis=0, tiled=True)
+    cot_full = lax.all_gather(cot_rows, "tensor", axis=0, tiled=True)
 
     gate_in = dot_wide(normed, w_gate)
     side_out = dot_wide(normed, w_side)
@@ -404,15 +443,11 @@
     group = max(1, LENGTH // token_count)
     if data_count % group:
         group = data_count
-    lines = [list(range(i, i + group)) for i in range(0, data_count, group)]
     mine = data_index % group
-
-    def gather_line(array):
-        return lax.all_gather(array, "dp", axis_index_groups=lines)
 
     device_decay = jnp.repeat(inflow[-1].reshape(heads_here, head_size)[:, :1], state_size, axis=1)
     sent = jnp.concatenate([local_end.astype(low), pad_to(device_decay, 16, 0).astype(low)])
-    arrived = gather_line(sent)
+    arrived = spread(sent, "dp", group, 1)
     decays = jnp.repeat(
         arrived[:, inner_here : inner_here + heads_here].astype(jnp.float32), head_size, axis=1
     )
@@ -434,63 +469,66 @@
     normed_out = (gated_normed * local_gate_gain).astype(low)
     d_gated = rstd_gate * scaled - gated * rstd_gate**3 * gate_dots
     d_mixed = d_gated * gate_act
-    state_cot = dot_wide((d_mixed * inflow).T.astype(low), state_c)
-    cots = gather_line(state_cot.astype(low))
+    d_gate_in = (d_gated * mixed * sigm * (1.0 + gate_in * (1.0 - sigm))).astype(low)
+    branch = dot_wide(normed_out, w_out.T).astype(low)
+    g_out = dot_wide(cot_full.T, normed_out).astype(low)
+    state_cot = dot_wide((d_mixed * inflow).T.astype(low), state_c).astype(low)
+    branch, g_out, state_cot = lax.optimization_barrier((branch, g_out, state_cot))
+    branch = lax.psum_scatter(branch, "tensor", scatter_dimension=0, tiled=True)
+    result = block_input + branch.astype(jnp.float32)
+    g_out = lax.psum_scatter(g_out, "dp", scatter_dimension=0, tiled=True)
+    cots = spread(state_cot, "dp", group, 2)
     leave_cot = chain(cots, decays, mine, True)
-    branch = lax.psum_scatter(
-        dot_wide(normed_out, w_out.T).astype(low), "tensor", scatter_dimension=0, tiled=True
-    )
-    result = block_input + branch.astype(jnp.float32)
-    g_out = dot_wide(cot_full.T, normed_out).astype(low)
-    g_out = lax.psum_scatter(g_out, "dp", scatter_dimension=0, tiled=True)
     g_gate_local = jnp.sum(d_normed_out * gated_normed, axis=0)
-    d_gate_in = (d_gated * mixed * sigm * (1.0 + gate_in * (1.0 - sigm))).astype(low)
     g_skip_wide = jnp.sum(d_mixed * x_wide, axis=0)
     g_skip_local = jnp.sum(g_skip_wide.reshape(heads_here, head_size), axis=1)
+    g_gate_in = dot_wide(normed.T, d_gate_in).astype(low)
+    leave_cot, g_gate_in = lax.optimization_barrier((leave_cot, g_gate_in))
+    g_gate_in = lax.psum_scatter(g_gate_in, "dp", scatter_dimension=0, tiled=True)
 
     d_x, d_b, d_c, dcum, colt, const, sx = scan_backward(
         inner_x, state_b, state_c, d_mixed, *scan_args, skip_wide, entry_state, leave_cot,
         heads=heads_here,
     )
     d_bc = lax.psum(jnp.concatenate([d_b, d_c], axis=1).astype(low), "tensor")
-    d_step, d_log = step_gradients(dcum, colt, const, sx, step_dt, log_decay, rate)
-    d_activ = jnp.concatenate([d_x, d_bc.astype(jnp.float32)], axis=1)
+    d_step, d_log = step_gradients(dcum, colt, const, sx, log_decay, rate)
+    ext_x, ext_bc = pre_ext[:, :inner_here], pre_ext[:, inner_here:]
 
     def conv_part(values, kernel, offsets):
         return conv_apply(values, kernel, offsets, validity)
 
-    conv_out, conv_back = jax.vjp(conv_part, pre_ext, conv_weight, conv_bias)
-    d_pre_ext, g_conv_w, g_conv_b = conv_back(d_activ)
-    from_next = from_behind(d_pre_ext[:width_back], "dp", -1)
-    d_pre_own = d_pre_ext[width_back:]
-    d_pre = jnp.concatenate(
-        [d_pre_own[:tail_start], d_pre_own[tail_start:] + from_next], axis=0
-    ).astype(low)
+    def shifted_back(ext, cols, d_out, axis_name):
+        _, back = jax.vjp(conv_part, ext, conv_weight[:, cols], conv_bias[cols])
+        d_ext, d_kernel, d_offsets = back(d_out)
+        from_next = from_behind(d_ext[:width_back], axis_name, -1)
+        own = d_ext[width_back:]
+        own = jnp.concatenate([own[:tail_start], own[tail_start:] + from_next], axis=0)
+        return own.astype(low), d_kernel, d_offsets
+
+    d_mix, g_cxw_local, g_cxb_local = shifted_back(ext_x, slice(0, inner_here), d_x, "dp")
+    d_pre_bc, g_cbw_local, g_cbb_local = shifted_back(
+        ext_bc, slice(inner_here, None), d_bc.astype(jnp.float32), "dp"
+    )
     d_raw = d_step * jax.nn.sigmoid(raw_dt)
     g_dt_bias_local = jnp.sum(d_raw, axis=0)
     d_raw_b = d_raw.astype(low)
-    d_mix = d_pre[:, :inner_here]
-    d_side = jnp.concatenate([d_pre[:, inner_here:], d_raw_b], axis=1)
+    d_side = jnp.concatenate([d_pre_bc, d_raw_b], axis=1)
     partial_rows = (
         dot_wide(d_gate_in, w_gate.T)
         + dot_wide(d_mix, w_mix.T)
         + dot_wide(d_raw_b, w_side[:, bc_size : bc_size + PAD].T)
     )
-    own_bc = lax.dynamic_slice_in_dim(d_pre[:, inner_here:], tensor_index * row_count, row_count, 0)
+    own_bc = lax.dynamic_slice_in_dim(d_pre_bc, tensor_index * row_count, row_count, 0)
     d_normed_rows = lax.psum_scatter(
         partial_rows.astype(low), "tensor", scatter_dimension=0, tiled=True
     ).astype(jnp.float32) + dot_wide(own_bc, w_side[:, :bc_size].T)
-    g_in = jnp.stack(
-        [
-            dot_wide(normed.T, d_gate_in),
-            dot_wide(normed.T, d_mix),
-            pad_to(dot_wide(normed.T, d_side), inner_here, 1),
-        ]
-    ).astype(low)
-    g_in = lax.psum_scatter(g_in, "dp", scatter_dimension=1, tiled=True).astype(jnp.float32)
-    grad_zx = g_in[:2]
-    grad_bc = g_in[2, :, :bc_size]
-    grad_dt = g_in[2, :, bc_size : bc_size + heads_here]
+    g_in = dot_wide(normed.T, jnp.concatenate([d_mix, d_side], axis=1)).astype(low)
+    g_in = pad_to(g_in, -(-g_in.shape[1] // 128) * 128, 1)
+    g_in = lax.psum_scatter(g_in, "dp", scatter_dimension=0, tiled=True).astype(jnp.float32)
+    grad_zx = jnp.stack([g_gate_in.astype(jnp.float32), g_in[:, :inner_here]])
+    side_end = inner_here + bc_size
+    grad_bc = g_in[:, inner_here:side_end]
+    grad_dt = g_in[:, side_end : side_end + heads_here]
     grad_out = g_out.astype(jnp.float32).T
     scaled_in = norm_gain * d_normed_rows
     g_norm_local = jnp.sum(d_normed_rows * block_input * rstd, axis=0)
@@ -500,26 +538,30 @@
         - block_input * rstd**3 * jnp.mean(scaled_in * block_input, axis=-1, keepdims=True)
     )
     pieces = (
+        g_cxw_local,
+        g_cxb_local,
+        g_gate_local,
+        g_dt_bias_local[:heads_here],
+        d_log[:heads_here],
+        g_skip_local,
         g_norm_local,
-        place_slice(g_conv_w[:, :inner_here], inner_total, inner_start, 1),
-        place_slice(g_conv_b[:inner_here], inner_total, inner_start, 0),
-        g_conv_w[:, inner_here:] / tensor_count,
-        g_conv_b[inner_here:] / tensor_count,
-        place_slice(g_dt_bias_local[:heads_here], heads_total, head_start, 0),
-        place_slice(d_log[:heads_here], heads_total, head_start, 0),
-        place_slice(g_skip_local, heads_total, head_start, 0),
-        place_slice(g_gate_local, inner_total, inner_start, 0),
+        g_cbw_local,
+        g_cbb_local,
     )
     flat = jnp.concatenate([piece.reshape(-1) for piece in pieces])
-    flat = pad_to(flat, -(-flat.shape[0] // 1024) * 1024, 0)
-    flat = lax.psum(flat, ("dp", "tensor"))
+    flat = pad_to(flat, -(-flat.shape[0] // 1024) * 1024, 0).reshape(-1, 128)
+    flat = jnp.sum(spread(flat, "dp", data_count, 3), axis=0)
+    flat = spread(flat, "tensor", tensor_count, 4).reshape(tensor_count, -1)
     small, at = [], 0
     for piece in pieces:
-        small.append(flat[at : at + piece.size].reshape(piece.shape))
+        small.append(flat[:, at : at + piece.size].reshape((tensor_count,) + piece.shape))
         at += piece.size
-    grad_norm, grad_cxw, grad_cxb, grad_cbw, grad_cbb, grad_dtb, grad_log, grad_skip, grad_gate = (
-        small
-    )
+    grad_cxw = jnp.moveaxis(small[0], 0, 1).reshape(-1, inner_total)
+    grad_cxb, grad_gate, grad_dtb, grad_log, grad_skip = [
+        part.reshape(-1) for part in small[1:6]
+    ]
+    grad_norm = jnp.sum(small[6], axis=0)
+    grad_cbw, grad_cbb = small[7][0], small[8][0]
     return (
         result,
         grad_input,
@@ -575,6 +617,7 @@
         P(),
         P("tensor", "dp"),
     )
+
     return jax.shard_map(
         per_device, mesh=mesh, in_specs=in_specs, out_specs=out_specs, check_vma=False
     )

time: 435 us -> 523 us (1.20)
  waiting for transfers between devices: 200 us -> 292 us
  blocking collectives: 72 us -> 39.6 us
  Pallas kernels: 31.3 us -> 62.1 us
  other arithmetic: 32.3 us -> 44.7 us
  matrix products: 40.6 us -> 32.8 us
  local copies, waits for them, and re-layouts: 38.1 us -> 30.4 us
    reduce_scatter x1 -> x2, waiting for transfers between devices: 0.01 us -> 69.6 us  [the longest x1 63.9 us: per_device(): g_out = lax.psum_scatter(g_out, 'dp', scatter_dimension=0, tiled=True)]
    psum x1 -> x0, blocking collectives: 39.7 us -> none  [per_device(): flat = lax.psum(flat, ('dp', 'tensor'))]
    unnamed x10 -> x11, waiting for transfers between devices: 76.4 us -> 112 us
    pallas_call x0 -> x4, Pallas kernels: none -> 31.1 us  [spread(): pl.pallas_call(functools.partial(spread_kernel, axis, group), out_shape=j...]
    unnamed x143 -> x171, local copies, waits for them, and re-layouts: 25.3 us -> 14.4 us
    dot_general x15 -> x14, matrix products: 40.3 us -> 32.5 us  [dot_wide(): return jnp.dot(left, right, preferred_element_type=jnp.float32)]
    psum x1, waiting for transfers between devices: 20.4 us -> 13.3 us  [per_device(): d_bc = lax.psum(jnp.concatenate([d_b, d_c], axis=1).astype(low), 'tensor')]
    all_gather x2 -> x1, blocking collectives: 26.6 us -> 33.6 us  [per_device(): w_out = lax.all_gather(out_part, 'dp', axis=0, tiled=True)]
  transfers between devices with their start and end apart: 10 -> 12, of which waited for: 7 -> 9; matrix products, arithmetic and copies ran while one was open for 18% -> 12% of each run, Pallas kernels for 2% -> 6%
where the time goes in v2:
time: 523 us; the launch traced here: 522 us
  waiting for transfers between devices  292 us (56%)
  Pallas kernels  62.1 us (12%)
  other arithmetic  44.7 us (9%)
  blocking collectives  39.6 us (8%)
  matrix products  32.8 us (6%)
  local copies, waits for them, and re-layouts  30.4 us (6%)
  between operations  15.2 us (3%)
  starting transfers between devices  5.63 us (1%)
    unnamed x11, waiting for transfers between devices  112 us
    reduce_scatter x1, waiting for transfers between devices, per_device(): g_out = lax.psum_scatter(g_out, 'dp', scatter_dimension=0, tiled=True)  63.9 us
    all_gather x1, waiting for transfers between devices, per_device(): every = lax.all_gather(packed, 'dp', axis=1, tiled=True)  48.7 us
    all_gather x1, blocking collectives, per_device(): w_out = lax.all_gather(out_part, 'dp', axis=0, tiled=True)  33.6 us
    dot_general x14, matrix products, dot_wide(): return jnp.dot(left, right, preferred_element_type=jnp.float32)  32.5 us
    pallas_call x4, Pallas kernels, spread(): pl.pallas_call(functools.partial(spread_kernel, axis, group), out_shape=j...  31.1 us
    reduce_scatter x1, waiting for transfers between devices, per_device(): lax.psum_scatter(partial_rows.astype(low), 'tensor', scatter_dimension=0,...  26.2 us
    pallas_call x1, Pallas kernels, scan_backward(): pl.pallas_call(functools.partial(scan_backward_kernel, heads, inner // he...  21.3 us
  transfers between devices with their start and end apart: 12, of which 9 were waited for; matrix products, arithmetic and copies ran while one was open for 12% of the time, Pallas kernels for 6%

profile of v2, /device:TPU:0, one launch (start us, length us, event | category | flops | bytes accessed | tf_op | source)
XLA Modules:
  0.0 521.9 jit_solution(3842724123517261444)
XLA Ops:
  16.3 17.6 %all-gather.6.cloned.1.call-done = bf16[1024,768]{1,0:T(8,128)(2,1)} async-done(((bf16[256,768]{1,0:T(8,128)(2,1)}), bf16[1024,768]{1,0:T(8,128)(2,1)}) %all-gather.6.cloned.1.call-update) | async-done | bytes 1572880 | tf_op jit(solution)/shard_map/all_gather | solution.py:391
  33.9 48.7 %all-gather.4.cloned.1.call-done = bf16[3,768,384]{2,1,0:T(8,128)(2,1)} async-done(((bf16[3,96,384]{2,1,0:T(8,128)(2,1)}), bf16[3,768,384]{2,1,0:T(8,128)(2,1)}) %all-gather.4.cloned.1.call-update) | async-done | bytes 1769488 | tf_op jit(solution)/shard_map/all_gather | solution.py:396
  82.5 2.5 fusion.91
  86.1 2.1 fusion.34
  88.5 2.5 collective-permute-start
  91.0 33.6 %all_gather.15 = bf16[768,384]{1,0:T(8,128)(2,1)} all-gather(bf16[96,384]{1,0:T(8,128)(2,1)S(1)} %bitcast.181), channel_id=1, replica_groups=mesh['dp'=8,'tensor'=4] {'dp'}, dimensions={0}, use_global_device_ids=true | all-gather | bytes 663552 | tf_op jit(solution)/shard_map/all_gather | solution.py:401
  127.6 2.5 multiply_convert_fusion
  132.7 9.7 %scan_forward.1 = (f32[1024,384]{1,0:T(8,128)S(1)}, f32[384,128]{1,0:T(8,128)S(1)}, f32[1024,384]{1,0:T(8,128)S(1)}) custom-call(bf16[1024,384]{1,0:T(8,128)(2,1)S(1)} %slice.409.x_ref, bf16[1024,128]{1,0:T(8,128)(2,1)S(1)} %get-tuple-element.166.b_ref, bf16[1024,128]{1,0:T(8,128)(2,1)S(1)} %get-tuple-element.165.c_ref, f32[1024,8]{1,0:T(8,128)S(1)} %copy.106.dt_ref, ...), custom_call_target="tpu_custom_call" | custom-call | tf_op jit(solution)/shard_map/scan_forward/pallas_call | solution.py:204
  146.1 7.5 %shard_map.271 = bf16[4,400,128]{2,1,0:T(8,128)(2,1)} custom-call(bf16[400,128]{1,0:T(8,128)(2,1)} %pad_maximum_fusion.3.own_ref), custom_call_target="tpu_custom_call" | custom-call | tf_op jit(solution)/shard_map/pallas_call | solution.py:288
  155.4 3.4 fusion.8
  159.5 5.3 %multiply_reduce_fusion.6 = (f32[1024]{0:T(1024)S(1)}, f32[1024]{0:T(1024)S(1)}, f32[1024,384]{1,0:T(8,128)}, f32[1024,384]{1,0:T(8,128)}) fusion(f32[384]{0:T(512)S(1)} %dynamic_slice.26, f32[1024,384]{1,0:T(8,128)} %fusion.8, f32[1024,384]{1,0:T(8,128)} %fusion.34, bf16[1024,768]{1,0:T(8,128)(2,1)} %all-gather.8.cloned.1.call-done, ...), kind=kOutput, calls=%fused_computation.45 | convolution fusion | flops 607909888 | bytes 8463872 | tf_op jit(solution)/shard_map/dot_general | solution.py:16
  164.8 5.9 %psum.14 = f32[2,1024]{1,0:T(2,128)S(1)} all-reduce(f32[2,1024]{1,0:T(2,128)S(1)} %pad_maximum_fusion.4), channel_id=1, replica_groups=mesh['dp'=8,'tensor'=4] {'tensor'}, use_global_device_ids=true, to_apply=%region_3.4 | all-reduce | flops 2048 | bytes 16384 | tf_op jit(solution)/shard_map/psum | solution.py:465
  170.8 3.8 convolution_convert_fusion
  174.6 5.0 fusion.9
  179.6 2.4 convolution_convert_fusion.4.own_ref
  184.0 9.2 %shard_map.272 = bf16[4,384,128]{2,1,0:T(8,128)(2,1)} custom-call(bf16[384,128]{1,0:T(8,128)(2,1)} %convolution_convert_fusion.4.own_ref), custom_call_target="tpu_custom_call" | custom-call | tf_op jit(solution)/shard_map/pallas_call | solution.py:288
  193.3 3.5 convolution_convert_fusion.2
  197.9 21.3 %scan_backward.1 = (f32[1024,384]{1,0:T(8,128)}, f32[1024,128]{1,0:T(8,128)S(1)}, f32[1024,128]{1,0:T(8,128)S(1)}, f32[1024,8]{1,0:T(8,128)S(1)}, f32[8,1024]{1,...) custom-call(bf16[1024,384]{1,0:T(8,128)(2,1)S(1)} %slice.409.x_ref, bf16[1024,128]{1,0:T(8,128)(2,1)S(1)} %copy-done.5, ...), custom_call_target="tpu_custom_call" | custom-call | tf_op jit(solution)/shard_map/scan_backward/pallas_call | solution.py:224
  223.2 6.4 %multiply_reduce_fusion.4 = (f32[384]{0:T(512)}, f32[384]{0:T(512)}, f32[384]{0:T(512)}, f32[384]{0:T(512)}, f32[384]{0:T(512)}, /*index=5*/f32[1024,384]{1,0:T(8,128)S(1)}) fusion(f32[1027,640]{1,0:T(8,128)} %copy-done.15, f32[1024]{0:T(1024)S(1)} %bitcast.166, f32[1024]{0:T(1024)S(1)} %bitcast.171, f32[1024]{0:T(1024)S(1)} %bitcast.176, ...), kind=kLoop, calls=%fused_computation.38 | loop fusion | flops 13367424 | bytes 9468928 | tf_op jit(solution)/shard_map/transpose(jvp())/reduce_sum | solution.py:317
  234.8 2.9 pad_add_fusion
  241.5 13.3 %all-reduce.24.cloned.1.call-done = bf16[1024,256]{1,0:T(8,128)(2,1)} async-done(((bf16[1024,256]{1,0:T(8,128)(2,1)}), bf16[1024,256]{1,0:T(8,128)(2,1)}) %all-reduce.24.cloned.1.call-update) | async-done | bytes 524304 | tf_op jit(solution)/shard_map/psum | solution.py:493
  254.8 3.8 multiply_reduce_fusion.10
  261.3 3.7 collective-permute-done.2
  271.2 2.2 add_convert_fusion
  274.6 46.2 %reduce-scatter.16.cloned.1.call-done = bf16[96,384]{1,0:T(8,128)(2,1)} async-done(((bf16[768,384]{1,0:T(8,128)(2,1)}), bf16[96,384]{1,0:T(8,128)(2,1)}) %reduce-scatter.16.cloned.1.call-update) | async-done | bytes 73744
  321.8 63.9 %reduce-scatter.14.cloned.1.call-done = bf16[96,384]{1,0:T(8,128)(2,1)} async-done(((bf16[768,384]{1,0:T(8,128)(2,1)}), bf16[96,384]{1,0:T(8,128)(2,1)}) %reduce-scatter.14.cloned.1.call-update) | async-done | bytes 73744 | tf_op jit(solution)/shard_map/reduce_scatter | solution.py:479
  387.3 65.5 %reduce-scatter.18.cloned.1.call-done = bf16[96,768]{1,0:T(8,128)(2,1)} async-done(((bf16[768,768]{1,0:T(8,128)(2,1)}), bf16[96,768]{1,0:T(8,128)(2,1)}) %reduce-scatter.18.cloned.1.call-update) | async-done | bytes 147472
  456.2 26.2 %reduce-scatter.12.cloned.1.call-done = bf16[256,768]{1,0:T(8,128)(2,1)} async-done(((bf16[1024,768]{1,0:T(8,128)(2,1)}), bf16[256,768]{1,0:T(8,128)(2,1)}) %reduce-scatter.12.cloned.1.call-update) | async-done | bytes 393232 | tf_op jit(solution)/shard_map/reduce_scatter | solution.py:522
  484.7 9.2 %shard_map.273 = f32[8,40,128]{2,1,0:T(8,128)} custom-call(f32[40,128]{1,0:T(8,128)} %pad_bitcast_fusion.own_ref), custom_call_target="tpu_custom_call" | custom-call | tf_op jit(solution)/shard_map/pallas_call | solution.py:288
  495.4 5.2 shard_map.274
  507.2 5.8 %reduce-scatter.10.cloned.1.call-done = bf16[256,768]{1,0:T(8,128)(2,1)} async-done(((bf16[1024,768]{1,0:T(8,128)(2,1)}), bf16[256,768]{1,0:T(8,128)(2,1)}) %reduce-scatter.10.cloned.1.call-update) | async-done | bytes 393232 | tf_op jit(solution)/shard_map/reduce_scatter | solution.py:477
  513.0 2.4 multiply_subtract_fusion.1
  (311 shorter events, 63.5 us)
Async XLA Ops:
  7.2 26.6 %all-gather.6.cloned.1.call-start = ((), (), s32[]{:S(2)}) async-start(), calls=%async_computation.6 | async-start | bytes 1966080 | tf_op jit(solution)/shard_map/all_gather | solution.py:391
  11.3 71.2 %all-gather.4.cloned.1.call-start = ((), (), s32[]{:S(2)}) async-start(), calls=%async_computation.5 | async-start | bytes 1990656 | tf_op jit(solution)/shard_map/all_gather | solution.py:396
  12.3 147.2 %all-gather.8.cloned.1.call-start = ((), (), s32[]{:S(2)}) async-start(), calls=%async_computation.7 | async-start | bytes 1966080 | tf_op jit(solution)/shard_map/all_gather | solution.py:402
  15.5 109.2 %copy-start.69 = (f32[8]{0:T(128)}, f32[8]{0:T(128)S(1)}, u32[]{:S(2)}) copy-start(f32[8]{0:T(128)S(1)} %pad.75) | copy-start | bytes 100
  16.2 108.4 %copy-start.71 = (f32[8]{0:T(128)}, f32[8]{0:T(128)S(1)}, u32[]{:S(2)}) copy-start(f32[8]{0:T(128)S(1)} %compare_select_fusion.1) | copy-start | bytes 100
  88.5 37.5 %collective-permute-start = (bf16[3,641]{1,0:T(4,128)(2,1)S(1)}, bf16[3,641]{1,0:T(4,128)(2,1)S(1)}, u32[]{:S(2)}, u32[]{:S(2)}) collective-permute-start(bf16[3,641]{1,0:T(4,128)(2,1)S(1)} %fusion.71), channel_id=1, source_target_pairs={{0,4},{4,8},{8,12},{12,16},{16,20},{20,24},{24,28},{1,5},{5,9},{9,... | collective-permute-start | bytes 11546 | tf_op jit(solution)/shard_map/ppermute | solution.py:308
  126.0 128.8 %all-reduce.24.cloned.1.call-start = ((), (), s32[]{:S(2)}) async-start(), calls=%async_computation.10 | async-start | bytes 1048576 | tf_op jit(solution)/shard_map/psum | solution.py:493
  221.3 99.5 %reduce-scatter.16.cloned.1.call-start = ((), (), s32[]{:S(2)}) async-start(), calls=%async_computation.12 | async-start | bytes 663552
  222.9 162.8 %reduce-scatter.14.cloned.1.call-start = ((), (), s32[]{:S(2)}) async-start(), calls=%async_computation.11 | async-start | bytes 663552 | tf_op jit(solution)/shard_map/reduce_scatter | solution.py:479
  232.7 7.8 %collective-permute-start.1 = (f32[3,384]{1,0:T(4,128)S(1)}, f32[3,384]{1,0:T(4,128)}, u32[]{:S(2)}, u32[]{:S(2)}) collective-permute-start(f32[3,384]{1,0:T(4,128)S(1)} %pad_add_fusion.2), channel_id=1, source_target_pairs={{4,0},{8,4},{12,8},{16,12},{20,16},{24,20},{28,24},{5,1},{9,5},{13... | collective-permute-start | bytes 13832 | tf_op jit(solution)/shard_map/ppermute | solution.py:308
  239.4 25.5 %copy-start.29 = (bf16[1021,384]{1,0:T(8,128)(2,1)}, bf16[1021,384]{1,0:T(8,128)(2,1)S(1)}, u32[]{:S(2)}) copy-start(bf16[1021,384]{1,0:T(8,128)(2,1)S(1)} %slice.592) | copy-start | bytes 2352388
  240.4 14.4 %copy-start.49 = (f32[1,256]{1,0:T(1,128)S(1)}, f32[1,256]{1,0:T(1,128)}, u32[]{:S(2)}) copy-start(f32[1,256]{1,0:T(1,128)} %get-tuple-element.193) | copy-start | bytes 3076
  240.4 14.4 %copy-start.50 = (f32[1,256]{1,0:T(1,128)S(1)}, f32[1,256]{1,0:T(1,128)}, u32[]{:S(2)}) copy-start(f32[1,256]{1,0:T(1,128)} %get-tuple-element.194) | copy-start | bytes 3076
  240.4 14.4 %copy-start.51 = (f32[1,256]{1,0:T(1,128)S(1)}, f32[1,256]{1,0:T(1,128)}, u32[]{:S(2)}) copy-start(f32[1,256]{1,0:T(1,128)} %get-tuple-element.195) | copy-start | bytes 3076
  240.5 14.3 %copy-start.63 = (f32[256]{0:T(256)S(1)}, f32[256]{0:T(256)}, u32[]{:S(2)}) copy-start(f32[256]{0:T(256)} %param.24) | copy-start | bytes 3076
  240.5 212.3 %reduce-scatter.18.cloned.1.call-start = ((), (), s32[]{:S(2)}) async-start(), calls=%async_computation.13 | async-start | bytes 1327104
  241.5 23.5 %copy-start.47 = (bf16[3,384]{1,0:T(4,128)(2,1)}, bf16[3,384]{1,0:T(4,128)(2,1)S(1)}, u32[]{:S(2)}) copy-start(bf16[3,384]{1,0:T(4,128)(2,1)S(1)} %fusion.70) | copy-start | bytes 6916
  259.5 5.5 %collective-permute-start.2 = (f32[3,256]{1,0:T(4,128)S(1)}, f32[3,256]{1,0:T(4,128)S(1)}, u32[]{:S(2)}, u32[]{:S(2)}) collective-permute-start(f32[3,256]{1,0:T(4,128)S(1)} %pad_add_fusion.4), channel_id=1, source_target_pairs={{4,0},{8,4},{12,8},{16,12},{20,16},{24,20},{28,24},{5,1},{9,5},{13... | collective-permute-start | bytes 9224 | tf_op jit(solution)/shard_map/ppermute | solution.py:308
  268.2 214.2 %reduce-scatter.12.cloned.1.call-start = ((), (), s32[]{:S(2)}) async-start(), calls=%async_computation.9 | async-start | bytes 1966080 | tf_op jit(solution)/shard_map/reduce_scatter | solution.py:522
  273.5 239.5 %reduce-scatter.10.cloned.1.call-start = ((), (), s32[]{:S(2)}) async-start(), calls=%async_computation.8 | async-start | bytes 1966080 | tf_op jit(solution)/shard_map/reduce_scatter | solution.py:477
  387.3 95.2 %copy-start.22 = (f32[256,768]{1,0:T(8,128)S(1)}, f32[256,768]{1,0:T(8,128)}, u32[]{:S(2)}) copy-start(f32[256,768]{1,0:T(8,128)} %param.16) | copy-start | bytes 2359300
  387.3 95.1 %copy-start.34 = (bf16[1021,256]{1,0:T(8,128)(2,1)S(1)}, bf16[1021,256]{1,0:T(8,128)(2,1)}, u32[]{:S(2)}) copy-start(bf16[1021,256]{1,0:T(8,128)(2,1)} %copy-done.33) | copy-start | bytes 1568260
  387.3 95.1 %copy-start.42 = (f32[768]{0:T(1024)S(1)}, f32[768]{0:T(1024)}, u32[]{:S(2)}) copy-start(f32[768]{0:T(1024)} %param.17) | copy-start | bytes 9220
  387.3 95.1 %copy-start.46 = (f32[256]{0:T(256)S(1)}, f32[256]{0:T(256)}, u32[]{:S(2)}) copy-start(f32[256]{0:T(256)} %copy-done.45) | copy-start | bytes 3076
  387.3 95.1 %copy-start.53 = (bf16[3,256]{1,0:T(4,128)(2,1)S(1)}, bf16[3,256]{1,0:T(4,128)(2,1)}, u32[]{:S(2)}) copy-start(bf16[3,256]{1,0:T(4,128)(2,1)} %copy-done.52) | copy-start | bytes 4612
  455.4 28.5 %copy-start.54 = (f32[384]{0:T(512)S(1)}, f32[384]{0:T(512)}, u32[]{:S(2)}) copy-start(f32[384]{0:T(512)} %get-tuple-element.138) | copy-start | bytes 4612
  455.4 28.5 %copy-start.59 = (f32[384]{0:T(512)S(1)}, f32[384]{0:T(512)}, u32[]{:S(2)}) copy-start(f32[384]{0:T(512)} %get-tuple-element.160) | copy-start | bytes 4612
  455.4 28.5 %copy-start.64 = (f32[256]{0:T(256)S(1)}, f32[256]{0:T(256)}, u32[]{:S(2)}) copy-start(f32[256]{0:T(256)} %get-tuple-element.141) | copy-start | bytes 3076
  455.4 28.5 %copy-start.73 = (f32[8]{0:T(128)S(1)}, f32[8]{0:T(128)}, u32[]{:S(2)}) copy-start(f32[8]{0:T(128)} %get-tuple-element.153) | copy-start | bytes 100
  455.4 28.5 %copy-start.74 = (f32[8]{0:T(128)S(1)}, f32[8]{0:T(128)}, u32[]{:S(2)}) copy-start(f32[8]{0:T(128)} %get-tuple-element.178) | copy-start | bytes 100
  456.2 56.8 %copy-start.26 = (f32[256,768]{1,0:T(8,128)S(1)}, f32[256,768]{1,0:T(8,128)}, u32[]{:S(2)}) copy-start(f32[256,768]{1,0:T(8,128)} %param.31) | copy-start | bytes 2359300
  456.2 56.8 %copy-start.61 = (f32[256]{0:T(256)S(1)}, f32[256]{0:T(256)}, u32[]{:S(2)}) copy-start(f32[256]{0:T(256)} %get-tuple-element.196) | copy-start | bytes 3076
  (60 other events, 197.3 us)
Sparse Core Ops, SparseCore 0:
  11.5 22.3 all-gather.5
  36.6 45.8 all-gather.3
  126.1 18.6 all-gather.7
  221.4 33.3 all-reduce.23
  257.9 62.8 reduce-scatter.15
  323.9 61.7 reduce-scatter.13
  389.1 63.6 reduce-scatter.17
  455.3 27.0 reduce-scatter.11
  484.9 28.0 reduce-scatter.9
